TPU v7x, 256 devices: a whole 4x4x8 slice. The times are simulated.
256 devices in a mesh: dp: 4 (over y), ctx: 64 (over x, z, core).
Axes of the slice: x: 4, y: 4, z: 8, core: 2. Of those that a mesh axis runs over, the one named last changes fastest.
Arguments:
- query_rows: bfloat16 [262144, 1024], P(('dp', 'ctx')), parts along dimension 0, may hold values from -6 to 6
- key_rows: bfloat16 [262144, 1024], P(('dp', 'ctx')), parts along dimension 0, may hold values from -6 to 6
- value_rows: bfloat16 [262144, 1024], P(('dp', 'ctx')), parts along dimension 0, may hold values from -6 to 6
- lengths: int32 [512], P('dp'), parts along dimension 0, may hold values from 1 to 40960, as said below
- conv_weight: float32 [3, 4, 1024], replicated, may hold values from -3 to 3
- out_gain: float32 [1024], replicated, may hold values from 0.1 to 1.9
Outputs:
- mixed: bfloat16 [262144, 1024], P(('dp', 'ctx')), parts along dimension 0
There are 4 independent parts, one for each index of `dp`. A program takes and returns all parts, laid end to end along the dimension named above; an argument that names none is the same for every part. Nothing has to cross between parts.
Inputs may be any that keep to these rules, and one draw needn't show every extreme that they name: The lengths of one part sum to 65536; the last document has exactly 40960 tokens.
All inputs are finite; a program needn't handle non-finite values.
Results may differ from a plain program's by a relative error of at most 0.0065.
Values may be sent and summed in bfloat16 or wider, within the bound.
No kernel may reach another device: no remote copies, remote signals or barrier semaphores. Data moves between devices by JAX's collectives and lax.ppermute only.
A program may use at most 128 MiB of HBM per device.

v0:
```python
import jax
import jax.numpy as jnp
from jax import lax
from jax.sharding import Mesh
from jax.sharding import PartitionSpec as P

HEAD = 128
CTX = ("ctx_0", "ctx_1", "ctx_2")
DP_CTX = ("dp", "ctx_0", "ctx_1", "ctx_2")


def from_behind(value, axis, steps):
    count = lax.axis_size(axis)
    leading, last = (max(0, -steps), min(count, count - steps))
    return lax.ppermute(value, axis, [(source, source + steps) for source in range(leading, last)])


def filled_with(array, identity):
    return jax.tree.map(
        lambda part, zero: jnp.zeros_like(part) + jnp.asarray(zero, part.dtype), array, identity
    )


def entering(array, axes, combine, identity):
    before = start = filled_with(array, identity)
    running = array
    for axis in reversed(axes):
        length, here = (lax.axis_size(axis), lax.axis_index(axis))
        pieces = jax.tree.map(lambda part: lax.all_gather(part, axis), running)
        inside, running = (start, start)
        for k in range(length):
            passed = k < here
            running = combine(running, jax.tree.map(lambda part: part[k], pieces))
            inside = jax.tree.map(lambda new, old: jnp.where(passed, new, old), running, inside)
        before = combine(inside, before)
    return before


def doc_lookup(starts, positions):
    return jnp.sum((starts[None, :] <= positions[:, None]).astype(jnp.int32), axis=1) - 1


def features(extended, doc_ext, conv_weight, row_count):
    made = []
    for which in range(3):
        summed = jnp.zeros((row_count, extended[which].shape[1]), jnp.float32)
        for delay in range(4):
            same_doc = (doc_ext[3 - delay : 3 - delay + row_count] == doc_ext[3:]).astype(
                jnp.float32
            )
            shifted = extended[which][3 - delay : 3 - delay + row_count].astype(jnp.float32)
            summed = summed + conv_weight[which, delay][None, :] * shifted * same_doc[:, None]
        made.append(summed)
    return (
        jax.nn.silu(made[0]).astype(jnp.bfloat16),
        jax.nn.silu(made[1]).astype(jnp.bfloat16),
        made[2].astype(jnp.bfloat16),
    )


def mix_block(query_part, key_part, value_part, state_bf, use_in, doc_ids, out_gain):
    row_count = query_part.shape[0]
    block = min(512, row_count)
    pieces = []
    for block_id in range(row_count // block):
        opening = block_id * block
        closing = opening + block
        scores = jnp.einsum(
            "qhd,khd->hqk",
            query_part[opening:closing],
            key_part[:closing],
            preferred_element_type=jnp.float32,
        )
        row_ids = jnp.arange(opening, closing)
        col_ids = jnp.arange(closing)
        allowed = (col_ids[None, :] <= row_ids[:, None]) & (
            doc_ids[:closing][None, :] == doc_ids[opening:closing][:, None]
        )
        weights = jnp.where(allowed[None], scores, 0.0).astype(jnp.bfloat16)
        within = jnp.einsum(
            "hqk,khe->qhe", weights, value_part[:closing], preferred_element_type=jnp.float32
        )
        carried = jnp.einsum(
            "qhd,hde->qhe",
            query_part[opening:closing],
            state_bf,
            preferred_element_type=jnp.float32,
        )
        pieces.append(within + carried * use_in[opening:closing, None, None])
    mixture = jnp.concatenate(pieces, axis=0)
    inverse_rms = lax.rsqrt(jnp.mean(mixture * mixture, axis=-1, keepdims=True) + 1e-06)
    normed = (mixture * inverse_rms).reshape(row_count, -1)
    return (normed * out_gain[None, :]).astype(jnp.bfloat16)


def join_states(earlier, later):
    merged = jnp.where(later[0][0] > 0, later[1], earlier[1] + later[1])
    return (jnp.maximum(earlier[0], later[0]), merged)


def per_device(query_rows, key_rows, value_rows, lengths, conv_weight, out_gain):
    row_count = query_rows.shape[0]
    channels = query_rows.shape[1]
    head_count = channels // HEAD
    offset = lax.axis_index(CTX) * row_count
    starts = jnp.cumsum(lengths) - lengths
    rims = from_behind(
        (query_rows[row_count - 3 :], key_rows[row_count - 3 :], value_rows[row_count - 3 :]),
        CTX,
        1,
    )
    extended = [
        jnp.concatenate([rims[0], query_rows], axis=0),
        jnp.concatenate([rims[1], key_rows], axis=0),
        jnp.concatenate([rims[2], value_rows], axis=0),
    ]
    positions = offset - 3 + jnp.arange(row_count + 3, dtype=jnp.int32)
    doc_ext = doc_lookup(starts, positions)
    phi_q, phi_k, val = features(extended, doc_ext, conv_weight, row_count)
    doc_ids = doc_ext[3:]
    phi_q = phi_q.reshape(row_count, head_count, HEAD)
    phi_k = phi_k.reshape(row_count, head_count, HEAD)
    val = val.reshape(row_count, head_count, HEAD)
    tail_mask = (doc_ids == doc_ids[-1]).astype(jnp.bfloat16)
    tail_state = jnp.einsum(
        "thd,the->hde", phi_k * tail_mask[:, None, None], val, preferred_element_type=jnp.float32
    )
    restart = (
        jnp.any((starts >= offset) & (starts < offset + row_count)).astype(jnp.float32).reshape(1)
    )
    identity = (jnp.zeros((1,), jnp.float32), jnp.zeros_like(tail_state))
    incoming = entering((restart, tail_state), CTX, join_states, identity)[1]
    opens_here = jnp.any(starts == offset)
    use_in = ((doc_ids == doc_ids[0]) & jnp.logical_not(opens_here)).astype(jnp.float32)
    return mix_block(phi_q, phi_k, val, incoming.astype(jnp.bfloat16), use_in, doc_ids, out_gain)


def solution(mesh):
    finer = Mesh(mesh.devices.reshape(mesh.shape["dp"], 4, 8, 2), ("dp", "ctx_0", "ctx_1", "ctx_2"))
    return jax.shard_map(
        per_device,
        mesh=finer,
        in_specs=(P(DP_CTX, None), P(DP_CTX, None), P(DP_CTX, None), P("dp"), P(), P()),
        out_specs=P(DP_CTX, None),
        check_vma=False,
    )
```

profile of v0, /device:TPU:8, one launch (start us, length us, event | category | flops | bytes accessed | tf_op | source)
XLA Modules:
  0.0 203.8 jit_solution(14183131050062450121)
XLA Ops:
  7.5 1.8 collective-permute-start.2
  10.2 4.1 %collective-permute-start = (bf16[3,1024]{0,1:T(8,128)(2,1)S(1)}, bf16[3,1024]{0,1:T(8,128)(2,1)S(1)}, u32[]{:S(2)}, u32[]{:S(2)}) collective-permute-start(bf16[3,1024]{0,1:T(8,128)(2,1)S(1)} %copy.77), channel_id=1, source_target_pairs={{0,1},{1,2},{2,3},{3,4},{4,5},{5,6},{6,7},{7,8},{8,9},{9,10},{10,1... | collective-permute-start | bytes 18440 | tf_op jit(solution)/shard_map/ppermute | solution.py:15
  15.4 1.4 compare_reduce_fusion
  19.4 1.3 and_convert_fusion
  20.8 3.9 %copy.83 = bf16[1024,1024]{0,1:T(8,128)(2,1)} copy(bf16[1024,1024]{1,0:T(8,128)(2,1)} %param.7) | data formatting | bytes 4194304 | tf_op args[1]
  24.7 2.9 %copy.76 = bf16[1024,1024]{0,1:T(8,128)(2,1)S(1)} copy(bf16[1024,1024]{1,0:T(8,128)(2,1)} %param.8) | data formatting | bytes 4194304 | tf_op args[2]
  27.6 9.0 %multiply_convert_fusion = bf16[1024,1024]{0,1:T(8,128)(2,1)S(1)} fusion(bf16[1024,1024]{0,1:T(8,128)(2,1)} %copy.83, bf16[3,1024]{0,1:T(8,128)(2,1)S(1)} %collective-permute-done.2, f32[1024]{0:T(1024)S(1)} %bitcast.178, f32[1024]{0:T(1024)S(1)} %bitcast.179, f32[1024]{0:T(1024)S(1)} %bitcast.176, f32[1024]{0:T(1024)S(1)} %bitcast.177, ...), kind=kLoop, calls=%fused_computation.9 | loop fusion | flops 29360128 | bytes 4229120 | tf_op jit(solution)/shard_map/convert_element_type | solution.py:56
  36.6 4.1 %add_convert_fusion = bf16[1024,1024]{0,1:T(8,128)(2,1)S(1)} fusion(bf16[1024,1024]{0,1:T(8,128)(2,1)S(1)} %copy.76, bf16[3,1024]{0,1:T(8,128)(2,1)S(1)} %collective-permute-done, f32[1024]{0:T(1024)S(1)} %get-tuple-element.26, f32[1024]{0:T(1024)S(1)} %bitcast.172, f32[1024]{0:T(1024)S(1)} %get-tuple-element.27, f32[1024]{0:T(1024)S(1)} %bitcast.173, ...), kind=kLoop, calls=%fused_computation.11 | loop fusion | flops 25165824 | bytes 4229120 | tf_op jit(solution)/shard_map/convert_element_type | solution.py:57
  42.0 1.5 fusion.15
  45.7 2.4 %all-reduce = f32[2]{0:T(128)S(1)} all-reduce(f32[2]{0:T(128)S(1)} %dynamic-update-slice), channel_id=1, replica_groups=mesh['dp'=4,'ctx_0'=4,'ctx_1'=8,'ctx_2'=2] {'ctx_2'}, use_global_device_ids=true, to_apply=%add | all-reduce | flops 2 | bytes 16
  49.5 10.5 %all-gather.11.cloned.1.call-done = f32[16,128,128]{2,1,0:T(8,128)} async-done(((f32[8,128,128]{2,1,0:T(8,128)}), f32[16,128,128]{2,1,0:T(8,128)}) %all-gather.11.cloned.1.call-update) | async-done | bytes 1048592 | tf_op jit(solution)/shard_map/all_gather | solution.py:29
  60.0 2.0 %add_select_fusion.19 = f32[1,8,128,128]{3,2,1,0:T(8,128)} fusion(f32[16,128,128]{2,1,0:T(8,128)} %all-gather.11.cloned.1.call-done, pred[]{:T(512)} %bitcast.31), kind=kLoop, calls=%fused_computation.64 | loop fusion | flops 262144 | bytes 1572865 | tf_op jit(solution)/shard_map/jit(_where)/select_n | solution.py:97
  62.8 1.4 dynamic-update-slice.1
  64.2 17.8 %all-reduce.1 = f32[8]{0:T(128)S(1)} all-reduce(f32[8]{0:T(128)S(1)} %dynamic-update-slice.1), channel_id=2, replica_groups=mesh['dp'=4,'ctx_0'=4,'ctx_1'=8,'ctx_2'=2] {'ctx_1'}, use_global_device_ids=true, to_apply=%add.1 | all-reduce | flops 8 | bytes 64
  87.1 31.3 %all-gather.7.cloned.1.call-done = f32[8,8,128,128]{3,2,1,0:T(8,128)} async-done(((f32[1,8,128,128]{3,2,1,0:T(8,128)}), f32[8,8,128,128]{3,2,1,0:T(8,128)}) %all-gather.7.cloned.1.call-update) | async-done | bytes 4194320 | tf_op jit(solution)/shard_map/all_gather | solution.py:29
  118.4 3.3 %add_select_fusion.4 = f32[1,8,128,128]{3,2,1,0:T(8,128)} fusion(f32[8,8,128,128]{3,2,1,0:T(8,128)} %all-gather.7.cloned.1.call-done, pred[]{:T(512)} %bitcast.49, pred[]{:T(512)} %bitcast.47, pred[]{:T(512)} %bitcast.45, pred[]{:T(512)} %bitcast.43, pred[]{:T(512)} %bitcast.41, pred[]{:T(512)} %bitcast.39, pred[]{:T(512)} %bitcast.35), kind=kLoop, calls=%fused_computation.49 | loop fusion | flops 1835008 | bytes 4718599 | tf_op jit(solution)/shard_map/jit(_where)/select_n | solution.py:97
  124.5 1.4 dynamic-update-slice.2
  126.0 1.6 collective-permute-start.1
  127.5 11.1 %all-reduce.2 = f32[4]{0:T(128)S(1)} all-reduce(f32[4]{0:T(128)S(1)} %dynamic-update-slice.2), channel_id=4, replica_groups=mesh['dp'=4,'ctx_0'=4,'ctx_1'=8,'ctx_2'=2] {'ctx_0'}, use_global_device_ids=true, to_apply=%add.2 | all-reduce | flops 4 | bytes 32
  142.9 2.9 %copy.80 = bf16[1024,1024]{0,1:T(8,128)(2,1)S(1)} copy(bf16[1024,1024]{1,0:T(8,128)(2,1)} %param.6) | data formatting | bytes 4194304 | tf_op args[0]
  152.7 2.3 %slice.339 = bf16[512,1024]{0,1:T(8,128)(2,1)} slice(bf16[1024,1024]{0,1:T(8,128)(2,1)} %copy-done.2), slice={[0:512], [0:1024]} | slice | bytes 2097152 | tf_op jit(solution)/shard_map/slice | solution.py:71
  155.0 2.3 %slice.328 = bf16[512,1024]{0,1:T(8,128)(2,1)} slice(bf16[1024,1024]{0,1:T(8,128)(2,1)} %copy-done.3), slice={[0:512], [0:1024]} | slice | bytes 2097152 | tf_op jit(solution)/shard_map/slice | solution.py:81
  157.3 4.5 %multiply_convert_fusion.1 = bf16[1024,1024]{0,1:T(8,128)(2,1)S(1)} fusion(bf16[1024,1024]{0,1:T(8,128)(2,1)S(1)} %copy.80, bf16[3,1024]{0,1:T(8,128)(2,1)S(1)} %collective-permute-done.1, f32[1024]{0:T(1024)S(1)} %bitcast.169, f32[1024]{0:T(1024)S(1)} %bitcast.170, f32[1024]{0:T(1024)S(1)} %bitcast.171, f32[1024]{0:T(1024)S(1)} %bitcast.168, ...), kind=kLoop, calls=%fused_computation.10 | loop fusion | flops 29360128 | bytes 4229120 | tf_op jit(solution)/shard_map/convert_element_type | solution.py:55
  162.1 4.4 %fusion.29 = bf16[8,128,128]{2,1,0:T(8,128)(2,1)S(1)} fusion(f32[4,8,128,128]{3,2,1,0:T(8,128)} %all-gather.9.cloned.1.call-done, f32[8,8,128,128]{3,2,1,0:T(8,128)} %all-gather.7.cloned.1.call-done, f32[16,128,128]{2,1,0:T(8,128)S(1)} %copy-done.4, pred[]{:T(512)S(6)} %gt.162, pred[]{:T(512)S(6)} %gt.161, pred[]{:T(512)S(6)} %gt.160, pred[]{:T(512)} %bitcast.57, ...), kind=kLoop, calls=%fused_computation.81 | loop fusion | flops 5373952 | bytes 7602203 | tf_op jit(solution)/shard_map/convert_element_type | solution.py:135
  166.5 1.8 fusion.41
  168.3 1.8 fusion.42
  170.1 8.5 %multiply_add_fusion = f32[8,128,512]{2,1,0:T(8,128)S(1)} fusion(f32[8,128,512]{2,1,0:T(8,128)} %fusion.42, bf16[1024,8,128]{0,2,1:T(8,128)(2,1)} %bitcast.161, bf16[512,8,128]{0,2,1:T(8,128)(2,1)} %bitcast.165, bf16[1024,8,128]{0,2,1:T(8,128)(2,1)} %bitcast.159, pred[512,1024]{1,0:T(8,128)(4,1)} %fusion.17, f32[512]{0:T(512)S(1)} %get-tuple-element.32), kind=kOutput, calls=%fused_computation.36 | convolution fusion | flops 2156920832 | bytes 9963520 | tf_op jit(solution)/shard_map/hqk,khe->qhe/dot_general | solution.py:80
  178.7 6.9 %multiply_add_fusion.1 = f32[8,128,512]{2,1,0:T(8,128)} fusion(f32[8,128,512]{2,1,0:T(8,128)} %fusion.41, bf16[512,8,128]{0,2,1:T(8,128)(2,1)} %bitcast.167, pred[512,512]{1,0:T(8,128)(4,1)S(1)} %copy-done.8, bf16[512,8,128]{0,2,1:T(8,128)(2,1)S(1)} %bitcast.163, bf16[512,8,128]{0,2,1:T(8,128)(2,1)} %bitcast.166, f32[512]{0:T(512)S(1)} %get-tuple-element.31), kind=kOutput, calls=%fused_computation.38 | convolution fusion | flops 1078984704 | bytes 7604224 | tf_op jit(solution)/shard_map/hqk,khe->qhe/dot_general | solution.py:80
  185.6 2.1 %fusion.3 = f32[1024,8]{0,1:T(8,128)S(1)} fusion(f32[512,8,128]{0,2,1:T(8,128)S(1)} %bitcast.154, f32[512,8,128]{0,2,1:T(8,128)} %bitcast.156), kind=kLoop, calls=%fused_computation.7 | loop fusion | flops 3137536 | bytes 4227072 | tf_op jit(solution)/shard_map/reduce_sum | solution.py:91
  188.0 1.9 copy.95
  189.9 3.1 %copy.96 = f32[512,1024]{1,0:T(8,128)} copy(f32[512,1024]{0,1:T(8,128)} %bitcast.155) | data formatting | bytes 4194304 | tf_op jit(solution)/shard_map/concatenate | solution.py:90
  194.6 2.7 %fusion.2 = bf16[1024,1024]{1,0:T(8,128)(2,1)} fusion(f32[128,8,8,128]{3,2,1,0:T(8,128)S(1)} %bitcast.153, f32[512,1024]{1,0:T(8,128)S(1)} %copy-done, f32[512,1024]{1,0:T(8,128)S(1)} %copy.95, f32[1024]{0:T(1024)S(1)} %copy-done.9), kind=kLoop, calls=%fused_computation.5 | loop fusion | flops 4194304 | bytes 10489856 | tf_op jit(solution)/shard_map/convert_element_type | solution.py:93
  (71 shorter events, 17.7 us)
Async XLA Ops:
  6.5 53.5 %all-gather.11.cloned.1.call-start = ((), (), s32[]{:S(2)}) async-start(), calls=%async_computation.2 | async-start | bytes 1572864 | tf_op jit(solution)/shard_map/all_gather | solution.py:29
  7.5 20.1 %collective-permute-start.2 = (bf16[3,1024]{0,1:T(8,128)(2,1)S(1)}, bf16[3,1024]{0,1:T(8,128)(2,1)S(1)}, u32[]{:S(2)}, u32[]{:S(2)}) collective-permute-start(bf16[3,1024]{0,1:T(8,128)(2,1)S(1)} %copy.84), channel_id=1, source_target_pairs={{0,1},{1,2},{2,3},{3,4},{4,5},{5,6},{6,7},{7,8},{8,9},{9,10},{10,1... | collective-permute-start | bytes 18440 | tf_op jit(solution)/shard_map/ppermute | solution.py:15
  10.2 26.4 %collective-permute-start = (bf16[3,1024]{0,1:T(8,128)(2,1)S(1)}, bf16[3,1024]{0,1:T(8,128)(2,1)S(1)}, u32[]{:S(2)}, u32[]{:S(2)}) collective-permute-start(bf16[3,1024]{0,1:T(8,128)(2,1)S(1)} %copy.77), channel_id=1, source_target_pairs={{0,1},{1,2},{2,3},{3,4},{4,5},{5,6},{6,7},{7,8},{8,9},{9,10},{10,1... | collective-permute-start | bytes 18440 | tf_op jit(solution)/shard_map/ppermute | solution.py:15
  36.6 4.2 %copy-start.2 = (bf16[1024,1024]{0,1:T(8,128)(2,1)}, bf16[1024,1024]{0,1:T(8,128)(2,1)S(1)}, u32[]{:S(2)}) copy-start(bf16[1024,1024]{0,1:T(8,128)(2,1)S(1)} %multiply_convert_fusion) | copy-start | bytes 6291460
  36.6 7.7 %copy-start.12 = (u32[256]{0:T(256)S(1)}, u32[256]{0:T(256)}, u32[]{:S(2)}) copy-start(u32[256]{0:T(256)} %constant.91) | copy-start | bytes 3076
  40.7 1.3 copy-start.3
  40.7 21.5 %copy-start.11 = (u32[256]{0:T(256)S(1)}, u32[256]{0:T(256)}, u32[]{:S(2)}) copy-start(u32[256]{0:T(256)} %constant.96) | copy-start | bytes 3076
  43.5 78.1 %copy-start.10 = (u32[256]{0:T(256)S(1)}, u32[256]{0:T(256)}, u32[]{:S(2)}) copy-start(u32[256]{0:T(256)} %constant.101) | copy-start | bytes 3076
  43.5 74.8 %all-gather.7.cloned.1.call-start = ((), (), s32[]{:S(2)}) async-start(), calls=%async_computation | async-start | bytes 4718592 | tf_op jit(solution)/shard_map/all_gather | solution.py:29
  62.1 99.9 %all-gather.9.cloned.1.call-start = ((), (), s32[]{:S(2)}) async-start(), calls=%async_computation.1 | async-start | bytes 2621440 | tf_op jit(solution)/shard_map/all_gather | solution.py:29
  126.0 31.4 %collective-permute-start.1 = (bf16[3,1024]{0,1:T(8,128)(2,1)S(1)}, bf16[3,1024]{0,1:T(8,128)(2,1)S(1)}, u32[]{:S(2)}, u32[]{:S(2)}) collective-permute-start(bf16[3,1024]{0,1:T(8,128)(2,1)S(1)} %copy.81), channel_id=1, source_target_pairs={{0,1},{1,2},{2,3},{3,4},{4,5},{5,6},{6,7},{7,8},{8,9},{9,10},{10,1... | collective-permute-start | bytes 18440 | tf_op jit(solution)/shard_map/ppermute | solution.py:15
  157.3 4.7 %copy-start.4 = (f32[16,128,128]{2,1,0:T(8,128)S(1)}, f32[16,128,128]{2,1,0:T(8,128)}, u32[]{:S(2)}) copy-start(f32[16,128,128]{2,1,0:T(8,128)} %all-gather.11.cloned.1.call-done) | copy-start | bytes 3145732
  162.0 6.3 %copy-start.5 = (bf16[512,1024]{0,1:T(8,128)(2,1)}, bf16[512,1024]{0,1:T(8,128)(2,1)S(1)}, u32[]{:S(2)}) copy-start(bf16[512,1024]{0,1:T(8,128)(2,1)S(1)} %get-tuple-element.8) | copy-start | bytes 3145732
  162.0 6.3 %copy-start.7 = (bf16[512,1024]{0,1:T(8,128)(2,1)}, bf16[512,1024]{0,1:T(8,128)(2,1)S(1)}, u32[]{:S(2)}) copy-start(bf16[512,1024]{0,1:T(8,128)(2,1)S(1)} %get-tuple-element.9) | copy-start | bytes 3145732
  170.1 8.5 %copy-start.6 = (bf16[512,1024]{0,1:T(8,128)(2,1)S(1)}, bf16[512,1024]{0,1:T(8,128)(2,1)}, u32[]{:S(2)}) copy-start(bf16[512,1024]{0,1:T(8,128)(2,1)} %copy-done.5) | copy-start | bytes 3145732
  170.1 8.5 %copy-start.8 = (pred[512,512]{1,0:T(8,128)(4,1)S(1)}, pred[512,512]{1,0:T(8,128)(4,1)}, u32[]{:S(2)}) copy-start(pred[512,512]{1,0:T(8,128)(4,1)} %fusion.19) | copy-start | bytes 786436
  178.6 7.0 %copy-start.1 = (f32[8,128,512]{2,1,0:T(8,128)}, f32[8,128,512]{2,1,0:T(8,128)S(1)}, u32[]{:S(2)}) copy-start(f32[8,128,512]{2,1,0:T(8,128)S(1)} %multiply_add_fusion) | copy-start | bytes 6291460
  189.9 4.3 %copy-start.9 = (f32[1024]{0:T(1024)S(1)}, f32[1024]{0:T(1024)}, u32[]{:S(2)}) copy-start(f32[1024]{0:T(1024)} %param.11) | copy-start | bytes 12292
  193.0 1.6 copy-start
Sparse Core Ops, SparseCore 0:
  43.7 16.3 all-gather.10
  62.2 56.0 all-gather.6
  121.8 31.9 all-gather.8
where the time goes:
time: 205 us; the launch traced here: 204 us
  waiting for transfers between devices  41.8 us (20%)
  other arithmetic  40.3 us (20%)
  local copies, waits for them, and re-layouts  34.2 us (17%)
  blocking collectives  31.4 us (15%)
  between operations  28 us (14%)
  matrix products  20.6 us (10%)
  starting transfers between devices  7.52 us (4%)
    all_gather x3, waiting for transfers between devices, entering(): pieces = jax.tree.map(lambda part: lax.all_gather(part, axis), running)  41.8 us
    unnamed x3, blocking collectives  31.4 us
    unnamed x38, local copies, waits for them, and re-layouts  17 us
    dot_general x2, matrix products, mix_block(): jnp.einsum('hqk,khe->qhe', weights, value_part[:closing], preferred_eleme...  15.4 us
    convert_element_type x1, other arithmetic, features(): jax.nn.silu(made[1]).astype(jnp.bfloat16)  9 us
    ppermute x3, starting transfers between devices, from_behind(): lax.ppermute(value, axis, [(source, source + steps) for source in range(l...  7.44 us
    select_n x2, other arithmetic, join_states(): merged = jnp.where(later[0][0] > 0, later[1], earlier[1] + later[1])  5.32 us
    concatenate x2, local copies, waits for them, and re-layouts, mix_block(): mixture = jnp.concatenate(pieces, axis=0)  5.03 us
  transfers between devices with their start and end apart: 6, of which 2 were waited for; matrix products, arithmetic and copies ran while one was open for 23% of the time, Pallas kernels for 0%

commit v1 on v0

v1 whole, which is shorter than its diff:
```python
import jax
import jax.numpy as jnp
from jax import lax
from jax.experimental import pallas as pl
from jax.experimental.pallas import tpu as pltpu
from jax.sharding import Mesh
from jax.sharding import PartitionSpec as P

HEAD = 128
PAIR = 2 * HEAD
CHUNK = 256
GROUP = 16
CTX = ("x", "z", "c")
DP_CTX = ("dp", "x", "z", "c")
F32 = jnp.float32
BF16 = jnp.bfloat16


def one_if(flag):
    return jnp.where(flag, 1.0, 0.0)


def starts_of(lengths):
    rows = jnp.broadcast_to(lengths, (8, HEAD))
    before = one_if(
        lax.broadcasted_iota(jnp.int32, (HEAD, HEAD), 0) < lax.broadcasted_iota(jnp.int32, (HEAD, HEAD), 1)
    ).astype(BF16)
    high = jnp.dot((rows >> 8).astype(F32).astype(BF16), before, preferred_element_type=F32)
    low = jnp.dot((rows & 255).astype(F32).astype(BF16), before, preferred_element_type=F32)
    return high * 256.0 + low


def docs_of(positions, starts):
    below = one_if(starts[0:1] <= positions.astype(F32)).astype(BF16)
    return jnp.dot(below, jnp.ones((HEAD, HEAD), BF16), preferred_element_type=F32), below


def wide(rows):
    return jnp.concatenate([rows, rows], axis=1)


def fill_doc(first, starts, doc_s, m_s):
    count = m_s.shape[1]
    iota = lax.broadcasted_iota(jnp.int32, (count + 8, HEAD), 0)
    doc, below = docs_of(iota + (first - 8), starts)
    doc_s[...] = doc
    for j in (1, 2, 3):
        m_s[j - 1] = one_if(doc_s[8 - j : 8 - j + count] == doc_s[8:])
    return below


def conv(ext, taps, m_s, r0):
    acc = taps[0:1] * ext[8 + r0 : 8 + r0 + CHUNK]
    for j in (1, 2, 3):
        acc += taps[j : j + 1] * (ext[8 + r0 - j : 8 + r0 - j + CHUNK] * m_s[j - 1, r0 : r0 + CHUNK])
    return acc


def silu_of_half(half):
    return half * jnp.tanh(half) + half


def kv_chunk(ext_k, ext_v, kw, vw, doc, m_s, r0):
    key = silu_of_half(conv(ext_k, kw, m_s, r0)).astype(BF16)
    val = conv(ext_v, vw, m_s, r0).astype(BF16)
    live = one_if(doc[8 + r0 : 8 + r0 + CHUNK] == doc[8 + r0 + CHUNK - 1 : 8 + r0 + CHUNK]).astype(BF16)
    tail = lax.dot_general(key * live, val, (((0,), (0,)), ((), ())), preferred_element_type=F32)
    return key, val, tail


def late_kernel(
    here_ref, len_ref, k_ref, v_ref, kw_ref, vw_ref,
    pk_ref, val_ref, st_ref, gate_ref, doc_s, m_s, ext_k, ext_v,
    *, chips,
):
    rows = k_ref.shape[0]
    chunks = rows // CHUNK

    @pl.when(pl.program_id(0) == 0)
    def _():
        here = here_ref[0]
        core = here % 2
        offset = here * rows
        starts = starts_of(len_ref[...])
        fill_doc(offset, starts, doc_s, m_s)
        chip = offset - core * rows
        first = (here // (2 * chips)) * (2 * chips * rows)
        mark = lax.broadcasted_iota(jnp.int32, (16, HEAD), 0)
        ends, _ = docs_of(first + mark * (2 * rows) - 1, starts)
        mine, _ = docs_of(chip + mark * rows - 1, starts)
        inner, _ = docs_of(offset + mark * CHUNK - 1, starts)
        keep_first = one_if(mine[1:2] == mine[0:1])
        keep_second = one_if(mine[2:3] == mine[1:2])
        second = jnp.full((1, HEAD), core, jnp.int32) == 1
        gate_ref[0:chips] = one_if(ends[1 : chips + 1] == ends[0:chips])
        one, zero = jnp.ones((1, HEAD), F32), jnp.zeros((1, HEAD), F32)
        rest = [
            jnp.where(second, one, keep_second),
            jnp.where(second, keep_second, one),
            jnp.where(second, keep_first, one),
            jnp.where(second, one, zero),
            jnp.where(second, one, keep_first),
            jnp.where(second, zero, one),
        ]
        for n, row in enumerate(rest):
            gate_ref[chips + n : chips + n + 1] = row
        for i in range(1, chunks):
            gate_ref[chips + 7 + i : chips + 8 + i] = one_if(inner[i : i + 1] == inner[0:1])
        for i in range(2, chunks + 1):
            gate_ref[chips + 9 + i : chips + 10 + i] = one_if(inner[i : i + 1] == inner[1:2])

    for n in (0, 1):
        cols = slice(n * HEAD, (n + 1) * HEAD)
        ext_k[n, CHUNK - 8 :] = k_ref[CHUNK - GROUP :, cols].astype(F32)
        ext_v[n, CHUNK - 8 :] = v_ref[CHUNK - GROUP :, cols].astype(F32)
    states = [jnp.zeros((HEAD, HEAD), F32)] * 2
    for i in range(1, chunks):
        r0 = i * CHUNK
        same = one_if(doc_s[8 + r0 - 1 : 8 + r0] == doc_s[8 + r0 + CHUNK - 1 : 8 + r0 + CHUNK])
        for n in (0, 1):
            cols = slice(n * HEAD, (n + 1) * HEAD)
            key, val, tail = kv_chunk(
                ext_k.at[n], ext_v.at[n], 0.5 * kw_ref[:, cols], vw_ref[:, cols], doc_s, m_s, r0
            )
            pk_ref[n, r0 - CHUNK : r0] = key
            val_ref[n, r0 - CHUNK : r0] = val
            states[n] = states[n] * same + tail
            st_ref[n, i - 1] = states[n]


def first_kernel(
    here_ref, len_ref, gate_ref, k_ref, v_ref, kr_ref, vr_ref, kw_ref, vw_ref, late_ref, *rest, rows, chips,
):
    pk_ref, val_ref, st_ref, tail_ref, doc_s, m_s, ext_k, ext_v = rest[-8:]
    count = late_ref.shape[1] + 1

    @pl.when(pl.program_id(0) == 0)
    def _():
        fill_doc(here_ref[0] * rows, starts_of(len_ref[...]), doc_s, m_s)

    for n in (0, 1):
        cols = slice(n * HEAD, (n + 1) * HEAD)
        ext_k[n, 0:8] = kr_ref[:, cols].astype(F32)
        ext_v[n, 0:8] = vr_ref[:, cols].astype(F32)
        ext_k[n, 8:] = k_ref[:, cols].astype(F32)
        ext_v[n, 8:] = v_ref[:, cols].astype(F32)
    for n in (0, 1):
        cols = slice(n * HEAD, (n + 1) * HEAD)
        pk_ref[n], val_ref[n], tail = kv_chunk(
            ext_k.at[n], ext_v.at[n], 0.5 * kw_ref[:, cols], vw_ref[:, cols], doc_s, m_s, 0
        )
        st_ref[n, 0] = tail.astype(BF16)
        for i in range(1, count):
            state = late_ref[n, i - 1] + tail * gate_ref[chips + 10 + i : chips + 11 + i]
            if i < count - 1:
                st_ref[n, i] = state.astype(BF16)
        tail_ref[n] = state.astype(BF16)


def attend_kernel(
    here_ref, len_ref, q_ref, qr_ref, qw_ref, pkf_ref, pkl_ref, valf_ref, vall_ref, *rest,
):
    pq_ref, mix_ref, doc_s, m_s, ext, allow_s = rest[-6:]
    rows = q_ref.shape[0]
    chunks = rows // CHUNK

    @pl.when(pl.program_id(0) == 0)
    def _():
        below = fill_doc(here_ref[0] * rows, starts_of(len_ref[...]), doc_s, m_s)
        across = lax.dot_general(
            jnp.ones((8, HEAD), BF16), below[8:], (((1,), (1,)), ((), ())), preferred_element_type=F32
        )
        causal = lax.broadcasted_iota(jnp.int32, (CHUNK, CHUNK), 1) <= lax.broadcasted_iota(
            jnp.int32, (CHUNK, CHUNK), 0
        )
        for i in range(chunks):
            r0 = i * CHUNK
            same = wide(doc_s[8 + r0 : 8 + r0 + CHUNK]) == across[0:1, r0 : r0 + CHUNK]
            allow_s[i] = jnp.where(same & causal, 1.0, 0.0).astype(BF16)

    for n in (0, 1):
        cols = slice(n * HEAD, (n + 1) * HEAD)
        ext[n, 0:8] = qr_ref[:, cols].astype(F32)
        ext[n, 8:] = q_ref[:, cols].astype(F32)

    def make(i, n):
        cols = slice(n * HEAD, (n + 1) * HEAD)
        r0 = i * CHUNK
        query = silu_of_half(conv(ext.at[n], 0.5 * qw_ref[:, cols], m_s, r0)).astype(BF16)
        use = one_if(doc_s[8 + r0 : 8 + r0 + CHUNK] == doc_s[8 + r0 - 1 : 8 + r0]).astype(BF16)
        pq_ref[n, r0 : r0 + CHUNK] = query * use
        return query

    def mixed(i, n, query):
        r0 = i * CHUNK
        key = pkf_ref[n] if i == 0 else pkl_ref[n, r0 - CHUNK : r0]
        val = valf_ref[n] if i == 0 else vall_ref[n, r0 - CHUNK : r0]
        scores = lax.dot_general(query, key, (((1,), (1,)), ((), ())), preferred_element_type=F32)
        weights = scores.astype(BF16) * allow_s[i]
        mix_ref[n, r0 : r0 + CHUNK] = jnp.dot(weights, val, preferred_element_type=F32).astype(BF16)

    order = [(i, n) for i in range(chunks) for n in (0, 1)]
    ahead = None
    for at in order:
        query = make(*at)
        if ahead is not None:
            mixed(*ahead)
        ahead = at + (query,)
    mixed(*ahead)


def finish_kernel(here_ref, gate_ref, mix_ref, pq_ref, st_ref, carried_ref, gain_ref, *rest, chips):
    out_ref = rest[-1]
    rows = pq_ref.shape[1]
    mean = jnp.full((HEAD, HEAD), 1.0 / HEAD, BF16)
    for n in (0, 1):
        carried = carried_ref[n].astype(F32)
        for i in range(rows // CHUNK):
            r0 = i * CHUNK
            state = carried
            if i:
                state = st_ref[n, i - 1].astype(F32) + carried * gate_ref[chips + 7 + i : chips + 8 + i]
            held = jnp.dot(pq_ref[n, r0 : r0 + CHUNK], state.astype(BF16), preferred_element_type=F32)
            mixture = mix_ref[n, r0 : r0 + CHUNK].astype(F32) + held
            square = jnp.dot((mixture * mixture).astype(BF16), mean, preferred_element_type=F32)
            scale = lax.rsqrt(square + 1e-06) * gain_ref[0:1, n * HEAD : (n + 1) * HEAD]
            out_ref[r0 : r0 + CHUNK, n * HEAD : (n + 1) * HEAD] = (mixture * scale).astype(BF16)


def rim_kernel(q_ref, k_ref, v_ref, out_ref):
    out_ref[0] = q_ref[...]
    out_ref[1] = k_ref[...]
    out_ref[2] = v_ref[...]


def join_kernel(gate_ref, own_ref, got_ref, out_ref, *, chips):
    own, got = gate_ref[chips : chips + 1], gate_ref[chips + 1 : chips + 2]
    out_ref[...] = (own_ref[...].astype(F32) * own + got_ref[...].astype(F32) * got).astype(BF16)


def total_kernel(gate_ref, spread_ref, out_ref):
    total = jnp.zeros(out_ref.shape, F32)
    for z in range(spread_ref.shape[0]):
        total = total * gate_ref[z : z + 1] + spread_ref[z].astype(F32)
    out_ref[...] = total


def enter_kernel(gate_ref, spread_ref, near_ref, far_ref, out_ref):
    running = near_ref[...] + far_ref[...]
    for z in range(spread_ref.shape[0]):
        out_ref[z] = running.astype(BF16)
        running = running * gate_ref[z : z + 1] + spread_ref[z].astype(F32)


def carry_kernel(gate_ref, entered_ref, own_ref, got_ref, mine_ref, other_ref, *, chips):
    gate = [gate_ref[chips + 2 + n : chips + 3 + n] for n in range(4)]
    entered = entered_ref[...].astype(F32)
    mine_ref[...] = (entered * gate[0] + got_ref[...].astype(F32) * gate[1]).astype(BF16)
    other_ref[...] = (entered * gate[2] + own_ref[...].astype(F32) * gate[3]).astype(BF16)


def in_hbm(x):
    return pltpu.with_memory_space_constraint(x, pltpu.HBM)


def params(mib):
    return pltpu.CompilerParams(dimension_semantics=("arbitrary",), vmem_limit_bytes=mib * 1024 * 1024)


def small(kernel, outs, *args):
    return pl.pallas_call(
        kernel, out_shape=outs, compiler_params=pltpu.CompilerParams(vmem_limit_bytes=4 * 1024 * 1024)
    )(*args)


def shaped(*shape, dtype=BF16):
    return jax.ShapeDtypeStruct(shape, dtype)


def per_device(query_rows, key_rows, value_rows, lengths, conv_weight, out_gain):
    query_rows, key_rows, value_rows, conv_weight = (
        in_hbm(x) for x in (query_rows, key_rows, value_rows, conv_weight)
    )
    rows, channels = query_rows.shape
    heads = channels // HEAD
    pairs = heads // 2
    half = heads // 2
    chunks = rows // CHUNK
    chips, x_count = lax.axis_size("z"), lax.axis_size("x")
    ctx_count = x_count * chips * 2
    here = lax.axis_index(CTX).astype(jnp.int32).reshape(1)
    swap = [(0, 1), (1, 0)]

    smem = pl.BlockSpec(memory_space=pltpu.SMEM)
    last_rows = pl.BlockSpec((8, channels), lambda i: (rows // 8 - 1, 0))
    rims = pl.pallas_call(
        rim_kernel,
        grid=(1,),
        in_specs=[last_rows] * 3,
        out_specs=pl.BlockSpec((3, 8, channels), lambda i: (0, 0, 0)),
        out_shape=shaped(3, 8, channels),
        compiler_params=params(4),
        name="rim",
    )(query_rows, key_rows, value_rows)
    rims = lax.ppermute(rims, CTX, [(i, i + 1) for i in range(ctx_count - 1)])

    whole = lambda *shape: pl.BlockSpec(shape, lambda p, *s: (0,) * len(shape))
    column = lambda count: pl.BlockSpec((count, PAIR), lambda p: (0, p))
    taps = lambda w: pl.BlockSpec((None, 4, PAIR), lambda p: (w, 0, p))
    two = lambda *shape: pl.BlockSpec((2,) + shape, lambda p: (p,) + (0,) * len(shape))
    anywhere = pl.BlockSpec(memory_space=pl.ANY)
    lengths = lengths.reshape(1, -1)
    gate_rows = 24
    half_pairs = pairs // 2

    def masks(count):
        return [pltpu.VMEM((count + 8, HEAD), F32), pltpu.VMEM((3, count, HEAD), F32)]

    pk_late, val_late, st_late, gates = pl.pallas_call(
        lambda *refs: late_kernel(*refs, chips=chips),
        grid=(pairs,),
        in_specs=[smem, whole(1, HEAD), column(rows), column(rows), taps(1), taps(2)],
        out_specs=[
            two(rows - CHUNK, HEAD),
            two(rows - CHUNK, HEAD),
            two(chunks - 1, HEAD, HEAD),
            whole(gate_rows, HEAD),
        ],
        out_shape=[
            pltpu.HBM((heads, rows - CHUNK, HEAD), BF16),
            pltpu.HBM((heads, rows - CHUNK, HEAD), BF16),
            shaped(heads, chunks - 1, HEAD, HEAD, dtype=F32),
            shaped(gate_rows, HEAD, dtype=F32),
        ],
        scratch_shapes=masks(rows) + [pltpu.VMEM((2, rows + 8, HEAD), F32)] * 2,
        compiler_params=params(20),
        name="late",
    )(here, lengths, key_rows, value_rows, conv_weight, conv_weight)
    pk_late, val_late = in_hbm(pk_late), in_hbm(val_late)

    def by_core(mine):
        pair = lambda p, s: p + ((s[0] % 2) if mine else (1 - s[0] % 2)) * half_pairs
        part = lambda *shape: pl.BlockSpec((2,) + shape, lambda p, s: (pair(p, s),) + (0,) * len(shape))
        cols = lambda count: pl.BlockSpec((count, PAIR), lambda p, s: (0, pair(p, s)))
        lead = lambda w, count: pl.BlockSpec((None, count, PAIR), lambda p, s: (w, 0, pair(p, s)))
        return part, cols, lead

    plain = lambda *shape: pl.BlockSpec((2,) + shape, lambda p, s: (p,) + (0,) * len(shape))

    def first(mine, *so_far):
        part, cols, lead = by_core(mine)
        args = (here, lengths, gates, key_rows, value_rows, rims, rims, conv_weight, conv_weight, st_late)
        return pl.pallas_call(
            lambda *refs: first_kernel(*refs, rows=rows, chips=chips),
            grid_spec=pltpu.PrefetchScalarGridSpec(
                num_scalar_prefetch=1,
                grid=(half_pairs,),
                in_specs=[
                    whole(1, HEAD),
                    whole(gate_rows, HEAD),
                    cols(CHUNK),
                    cols(CHUNK),
                    lead(1, 8),
                    lead(2, 8),
                    lead(1, 4),
                    lead(2, 4),
                    part(chunks - 1, HEAD, HEAD),
                ]
                + [anywhere] * len(so_far),
                out_specs=[
                    part(CHUNK, HEAD),
                    part(CHUNK, HEAD),
                    part(chunks - 1, HEAD, HEAD),
                    plain(HEAD, HEAD),
                ],
                scratch_shapes=masks(CHUNK) + [pltpu.VMEM((2, CHUNK + 8, HEAD), F32)] * 2,
            ),
            out_shape=[
                pltpu.HBM((heads, CHUNK, HEAD), BF16),
                pltpu.HBM((heads, CHUNK, HEAD), BF16),
                pltpu.HBM((heads, chunks - 1, HEAD, HEAD), BF16),
                shaped(half, HEAD, HEAD),
            ],
            input_output_aliases={len(args) + n: n for n in range(len(so_far))},
            compiler_params=params(8),
            name="first",
        )(*args, *so_far)

    *so_far, other = first(False)
    so_far = [in_hbm(x) for x in so_far]
    got = lax.ppermute(other, "c", swap)
    pk_first, val_first, inner, own = first(True, *so_far)
    pk_first, val_first, inner = in_hbm(pk_first), in_hbm(val_first), in_hbm(inner)

    state = (half, HEAD, HEAD)
    chip_tail = small(lambda *r: join_kernel(*r, chips=chips), pltpu.HBM(state, BF16), gates, own, got)
    spread = lax.all_to_all(chip_tail.reshape(chips, -1, HEAD), "z", 0, 0, tiled=True)

    def attend(pair, count, *so_far):
        at = lambda p: p + pair
        cols = lambda n: pl.BlockSpec((n, PAIR), lambda p: (0, at(p)))
        part = lambda *shape: pl.BlockSpec((2,) + shape, lambda p: (at(p),) + (0,) * len(shape))
        args = (here, lengths, query_rows, rims, conv_weight, pk_first, pk_late, val_first, val_late)
        return pl.pallas_call(
            attend_kernel,
            grid=(count,),
            in_specs=[
                smem,
                whole(1, HEAD),
                cols(rows),
                pl.BlockSpec((None, 8, PAIR), lambda p: (0, 0, at(p))),
                pl.BlockSpec((None, 4, PAIR), lambda p: (0, 0, at(p))),
                part(CHUNK, HEAD),
                part(rows - CHUNK, HEAD),
                part(CHUNK, HEAD),
                part(rows - CHUNK, HEAD),
            ]
            + [anywhere] * len(so_far),
            out_specs=[part(rows, HEAD), part(rows, HEAD)],
            out_shape=[pltpu.HBM((heads, rows, HEAD), BF16)] * 2,
            scratch_shapes=masks(rows)
            + [pltpu.VMEM((2, rows + 8, HEAD), F32), pltpu.VMEM((chunks, CHUNK, CHUNK), BF16)],
            input_output_aliases={len(args) + n: n for n in range(len(so_far))},
            compiler_params=params(20),
            name="attend",
        )(*args, *so_far)

    mixed = [in_hbm(x) for x in attend(0, half_pairs)]
    phi_q, mix = (in_hbm(x) for x in attend(half_pairs, half_pairs, *mixed))

    row_total = small(total_kernel, shaped(*spread.shape[1:], dtype=F32), gates, spread)
    far = lax.ppermute(row_total, "x", [(1, 3)])
    near = lax.ppermute(row_total, "x", [(i, i + 1) for i in range(x_count - 1)])
    entering = small(enter_kernel, pltpu.HBM(spread.shape, BF16), gates, spread, near, far)
    entered = lax.all_to_all(entering, "z", 0, 0, tiled=True).reshape(state)
    carried_own, carried_other = small(
        lambda *r: carry_kernel(*r, chips=chips), [shaped(*state)] * 2, gates, entered, own, got
    )
    carried_far = lax.ppermute(carried_other, "c", swap)

    def finish(mine, carried, *so_far):
        part, cols, _ = by_core(mine)
        args = (here, gates, mix, phi_q, inner, carried, out_gain.reshape(1, -1))
        return pl.pallas_call(
            lambda *refs: finish_kernel(*refs, chips=chips),
            grid_spec=pltpu.PrefetchScalarGridSpec(
                num_scalar_prefetch=1,
                grid=(half_pairs,),
                in_specs=[
                    whole(gate_rows, HEAD),
                    part(rows, HEAD),
                    part(rows, HEAD),
                    part(chunks - 1, HEAD, HEAD),
                    plain(HEAD, HEAD),
                    cols(1),
                ]
                + [anywhere] * len(so_far),
                out_specs=cols(rows),
            ),
            out_shape=shaped(rows, channels),
            input_output_aliases={len(args) + n: n for n in range(len(so_far))},
            compiler_params=params(16),
            name="finish",
        )(*args, *so_far)

    done = finish(True, carried_own)
    return finish(False, carried_far, done)


def solution(mesh):
    finer = Mesh(mesh.devices.reshape(mesh.shape["dp"], 4, 8, 2), DP_CTX)

    return jax.shard_map(
        per_device,
        mesh=finer,
        in_specs=(P(DP_CTX, None), P(DP_CTX, None), P(DP_CTX, None), P("dp"), P(), P()),
        out_specs=P(DP_CTX, None),
        check_vma=False,
    )
```

time: 205 us -> 76.5 us (0.37)
  the two profiles are of different devices: /device:TPU:8 before, /device:TPU:3 now
where the time goes in v1:
time: 76.5 us; the launch traced here: 75.9 us
  Pallas kernels  32.2 us (42%)
  blocking collectives  26.2 us (34%)
  starting transfers between devices  14.7 us (19%)
  waiting for transfers between devices  2.73 us (4%)
    all_to_all x1, blocking collectives, per_device(): lax.all_to_all(chip_tail.reshape(chips, -1, HEAD), 'z', 0, 0, tiled=True)  15.1 us
    all_to_all x1, blocking collectives, per_device(): entered = lax.all_to_all(entering, 'z', 0, 0, tiled=True).reshape(state)  11.2 us
    pallas_call x2, Pallas kernels, attend(): pl.pallas_call(attend_kernel, grid=(count,), in_specs=[smem, whole(1, HEA...  10.5 us
    pallas_call x1, Pallas kernels, per_device(): pl.pallas_call(lambda *refs: late_kernel(*refs, chips=chips), grid=(pairs...  7.05 us
    pallas_call x2, Pallas kernels, finish(): pl.pallas_call(lambda *refs: finish_kernel(*refs, chips=chips), grid_spec...  6.41 us
    pallas_call x2, Pallas kernels, first(): pl.pallas_call(lambda *refs: first_kernel(*refs, rows=rows, chips=chips),...  5.99 us
    ppermute x1, starting transfers between devices, per_device(): carried_far = lax.ppermute(carried_other, 'c', swap)  4.92 us
    ppermute x1, starting transfers between devices, per_device(): rims = lax.ppermute(rims, CTX, [(i, i + 1) for i in range(ctx_count - 1)])  4.09 us
  transfers between devices with their start and end apart: 5, of which 1 were waited for; matrix products, arithmetic and copies ran while one was open for 0% of the time, Pallas kernels for 31%

profile of v1, /device:TPU:3, one launch (start us, length us, event | category | flops | bytes accessed | tf_op | source)
XLA Modules:
  0.0 75.9 jit_solution(8499099710094464246)
XLA Ops:
  0.0 0.0 copy-start.1
  0.0 0.8 %rim.1 = bf16[3,8,1024]{2,1,0:T(8,128)(2,1)S(1)} custom-call(bf16[1024,1024]{1,0:T(8,128)(2,1)} %q_ref.5, bf16[1024,1024]{1,0:T(8,128)(2,1)} %refs_3_.5, bf16[1024,1024]{1,0:T(8,128)(2,1)} %refs_4_.5), custom_call_target="tpu_custom_call" | custom-call | tf_op jit(solution)/shard_map/rim/pallas_call | solution.py:296
  0.8 4.1 %collective-permute-start = (bf16[3,8,1024]{2,1,0:T(8,128)(2,1)S(1)}, bf16[3,8,1024]{2,1,0:T(8,128)(2,1)S(1)}, u32[]{:S(2)}, u32[]{:S(2)}) collective-permute-start(bf16[3,8,1024]{2,1,0:T(8,128)(2,1)S(1)} %rim.1), channel_id=1, source_target_pairs={{0,1},{1,2},{2,3},{3,4},{4,5},{5,6},{6,7},{7,8},{8,9},{9,10},{10,1... | collective-permute-start | bytes 147464 | tf_op jit(solution)/shard_map/ppermute | solution.py:305
  4.9 0.0 copy-done.1
  4.9 7.1 %late.1 = (bf16[8,768,128]{2,1,0:T(8,128)(2,1)}, bf16[8,768,128]{2,1,0:T(8,128)(2,1)}, f32[8,3,128,128]{3,2,1,0:T(8,128)S(1)}, f32[24,128]{1,0:T(8,128)S(1)}) custom-call(s32[1]{0:T(128)} %bitcast.refs_0_.here_ref, s32[1,128]{1,0:T(1,128)S(1)} %bitcast.8, bf16[1024,1024]{1,0:T(8,128)(2,1)} %refs_3_.5, bf16[1024,1024]{1,0:T(8,128)(2,1)} %refs_4_.5, ...), custom_call_target="tpu_custom_call" | custom-call | tf_op jit(solution)/shard_map/late/pallas_call | solution.py:319
  11.9 0.0 collective-permute-done.refs_5_.refs_6_.qr_ref
  11.9 3.0 %first.2 = (bf16[8,256,128]{2,1,0:T(8,128)(2,1)}, bf16[8,256,128]{2,1,0:T(8,128)(2,1)}, bf16[8,3,128,128]{3,2,1,0:T(8,128)(2,1)}, bf16[4,128,128]{2,1,0:T(8,128)(2,1)S(1)}) custom-call(s32[1]{0:T(128)} %bitcast.refs_0_.here_ref, s32[1,128]{1,0:T(1,128)S(1)} %bitcast.9, f32[24,128]{1,0:T(8,128)S(1)} %get-tuple-element.23.refs_2_.r_0_.gate_ref.refs_1_, ...), custom_call_target="tpu_custom_call" | custom-call | tf_op jit(solution)/shard_map/first/pallas_call | solution.py:353
  14.9 0.0 collective-permute-start.1
  14.9 3.0 %first.3 = (bf16[8,256,128]{2,1,0:T(8,128)(2,1)}, bf16[8,256,128]{2,1,0:T(8,128)(2,1)}, bf16[8,3,128,128]{3,2,1,0:T(8,128)(2,1)}, bf16[4,128,128]{2,1,0:T(8,128)(2,1)S(1)}) custom-call(s32[1]{0:T(128)} %bitcast.refs_0_.here_ref, s32[1,128]{1,0:T(1,128)S(1)} %bitcast.10, ...), custom_call_target="tpu_custom_call", output_to_operand_aliasing={{0}: (10, {}), {1}: (11, {}), {2}: (12, {})} | custom-call | tf_op jit(solution)/shard_map/first/pallas_call | solution.py:353
  17.9 0.0 collective-permute-done.1.r_2_.r_3_
  17.9 0.7 shard_map.64
  18.6 15.1 %all_to_all.10.spread_ref = bf16[8,64,128]{2,1,0:T(8,128)(2,1)S(1)} all-to-all(bf16[8,64,128]{2,1,0:T(8,128)(2,1)} %bitcast.13), channel_id=1, replica_groups=mesh['dp'=4,'x'=4,'z'=8,'c'=2] {'z'}, dimensions={0} | all-to-all | bytes 262144 | tf_op jit(solution)/shard_map/all_to_all | solution.py:397
  33.7 3.8 %collective-permute-start.3 = (f32[64,128]{1,0:T(8,128)S(1)}, f32[64,128]{1,0:T(8,128)S(1)}, u32[]{:S(2)}, u32[]{:S(2)}) collective-permute-start(f32[64,128]{1,0:T(8,128)S(1)} %shard_map.65), channel_id=1, source_target_pairs={{16,48},{17,49},{18,50},{19,51},{20,52},{21,53},{22,54},{23,55},{2... | collective-permute-start | bytes 98312 | tf_op jit(solution)/shard_map/ppermute | solution.py:432
  37.5 1.9 %collective-permute-start.2 = (f32[64,128]{1,0:T(8,128)S(1)}, f32[64,128]{1,0:T(8,128)S(1)}, u32[]{:S(2)}, u32[]{:S(2)}) collective-permute-start(f32[64,128]{1,0:T(8,128)S(1)} %shard_map.65), channel_id=1, source_target_pairs={{0,16},{16,32},{32,48},{1,17},{17,33},{33,49},{2,18},{18,34},{34,5... | collective-permute-start | bytes 98312 | tf_op jit(solution)/shard_map/ppermute | solution.py:433
  39.4 0.0 collective-permute-done.3.far_ref
  39.4 2.7 %collective-permute-done.2.near_ref = f32[64,128]{1,0:T(8,128)S(1)} collective-permute-done((f32[64,128]{1,0:T(8,128)S(1)}, f32[64,128]{1,0:T(8,128)S(1)}, u32[]{:S(2)}, u32[]{:S(2)}) %collective-permute-start.2) | collective-permute-done | bytes 32800 | tf_op jit(solution)/shard_map/ppermute | solution.py:433
  42.2 0.7 shard_map.66
  42.8 11.2 %all_to_all.11 = bf16[8,64,128]{2,1,0:T(8,128)(2,1)S(1)} all-to-all(bf16[8,64,128]{2,1,0:T(8,128)(2,1)} %shard_map.66), channel_id=1, replica_groups=mesh['dp'=4,'x'=4,'z'=8,'c'=2] {'z'}, dimensions={0} | all-to-all | bytes 262144 | tf_op jit(solution)/shard_map/all_to_all | solution.py:435
  54.0 0.1 shard_map.67
  54.1 4.9 %collective-permute-start.4 = (bf16[4,128,128]{2,1,0:T(8,128)(2,1)S(1)}, bf16[4,128,128]{2,1,0:T(8,128)(2,1)S(1)}, u32[]{:S(2)}, u32[]{:S(2)}) collective-permute-start(bf16[4,128,128]{2,1,0:T(8,128)(2,1)S(1)} %get-tuple-element.39), channel_id=1, source_target_pairs={{0,1},{1,0},{2,3},{3,2},{4,5},{5,4},{6,7},{7,6},{8,9},{9,8},{10,11... | collective-permute-start | bytes 393224 | tf_op jit(solution)/shard_map/ppermute | solution.py:439
  59.1 5.2 %attend.2 = (bf16[8,1024,128]{2,1,0:T(8,128)(2,1)}, bf16[8,1024,128]{2,1,0:T(8,128)(2,1)}) custom-call(s32[1]{0:T(128)} %bitcast.refs_0_.here_ref, s32[1,128]{1,0:T(1,128)S(1)} %bitcast.11, bf16[1024,1024]{1,0:T(8,128)(2,1)} %q_ref.5, bf16[3,8,1024]{2,1,0:T(8,128)(2,1)S(1)} %collective-permute-done.refs_5_.refs_6_.qr_ref, f32[3,4,1024]{2,1,0:T(4,128)} %qw_ref.3, ...), custom_call_target="tpu_custom_call" | custom-call | tf_op jit(solution)/shard_map/attend/pallas_call | solution.py:404
  64.3 0.0 copy-start
  64.3 5.2 %attend.3 = (bf16[8,1024,128]{2,1,0:T(8,128)(2,1)}, bf16[8,1024,128]{2,1,0:T(8,128)(2,1)}) custom-call(s32[1]{0:T(128)} %bitcast.refs_0_.here_ref, s32[1,128]{1,0:T(1,128)S(1)} %bitcast.12, bf16[1024,1024]{1,0:T(8,128)(2,1)} %q_ref.5, ...), custom_call_target="tpu_custom_call", output_to_operand_aliasing={{0}: (9, {}), {1}: (10, {})} | custom-call | tf_op jit(solution)/shard_map/attend/pallas_call | solution.py:404
  69.5 0.0 copy-done
  69.5 3.2 %finish.2.refs_7_ = bf16[1024,1024]{1,0:T(8,128)(2,1)} custom-call(s32[1]{0:T(128)} %bitcast.refs_0_.here_ref, f32[24,128]{1,0:T(8,128)S(1)} %get-tuple-element.23.refs_2_.r_0_.gate_ref.refs_1_, bf16[8,1024,128]{2,1,0:T(8,128)(2,1)} %get-tuple-element.34.refs_2_, bf16[8,1024,128]{2,1,0:T(8,128)(2,1)} %get-tuple-element.35.refs_3_, ...), custom_call_target="tpu_custom_call" | custom-call | tf_op jit(solution)/shard_map/finish/pallas_call | solution.py:444
  72.7 0.0 collective-permute-done.4.refs_5_
  72.7 3.2 %finish.3 = bf16[1024,1024]{1,0:T(8,128)(2,1)} custom-call(s32[1]{0:T(128)} %bitcast.refs_0_.here_ref, f32[24,128]{1,0:T(8,128)S(1)} %get-tuple-element.23.refs_2_.r_0_.gate_ref.refs_1_, bf16[8,1024,128]{2,1,0:T(8,128)(2,1)} %get-tuple-element.34.refs_2_, bf16[8,1024,128]{2,1,0:T(8,128)(2,1)} %get-tuple-element.35.refs_3_, ...), custom_call_target="tpu_custom_call", output_to_operand_aliasing={{}: (7, {})} | custom-call | tf_op jit(solution)/shard_map/finish/pallas_call | solution.py:444
  (1 shorter events, 0.0 us)
Async XLA Ops:
  0.0 4.9 %copy-start.1 = (s32[128]{0:T(128)S(1)}, s32[128]{0:T(128)}, u32[]{:S(2)}) copy-start(s32[128]{0:T(128)} %param.9) | copy-start | bytes 1540
  0.8 11.2 %collective-permute-start = (bf16[3,8,1024]{2,1,0:T(8,128)(2,1)S(1)}, bf16[3,8,1024]{2,1,0:T(8,128)(2,1)S(1)}, u32[]{:S(2)}, u32[]{:S(2)}) collective-permute-start(bf16[3,8,1024]{2,1,0:T(8,128)(2,1)S(1)} %rim.1), channel_id=1, source_target_pairs={{0,1},{1,2},{2,3},{3,4},{4,5},{5,6},{6,7},{7,8},{8,9},{9,10},{10,1... | collective-permute-start | bytes 147464 | tf_op jit(solution)/shard_map/ppermute | solution.py:305
  14.9 3.0 %collective-permute-start.1 = (bf16[4,128,128]{2,1,0:T(8,128)(2,1)S(1)}, bf16[4,128,128]{2,1,0:T(8,128)(2,1)S(1)}, u32[]{:S(2)}, u32[]{:S(2)}) collective-permute-start(bf16[4,128,128]{2,1,0:T(8,128)(2,1)S(1)} %get-tuple-element.38), channel_id=1, source_target_pairs={{0,1},{1,0},{2,3},{3,2},{4,5},{5,4},{6,7},{7,6},{8,9},{9,8},{10,11... | collective-permute-start | bytes 393224 | tf_op jit(solution)/shard_map/ppermute | solution.py:391
  33.7 5.7 %collective-permute-start.3 = (f32[64,128]{1,0:T(8,128)S(1)}, f32[64,128]{1,0:T(8,128)S(1)}, u32[]{:S(2)}, u32[]{:S(2)}) collective-permute-start(f32[64,128]{1,0:T(8,128)S(1)} %shard_map.65), channel_id=1, source_target_pairs={{16,48},{17,49},{18,50},{19,51},{20,52},{21,53},{22,54},{23,55},{2... | collective-permute-start | bytes 98312 | tf_op jit(solution)/shard_map/ppermute | solution.py:432
  37.5 4.7 %collective-permute-start.2 = (f32[64,128]{1,0:T(8,128)S(1)}, f32[64,128]{1,0:T(8,128)S(1)}, u32[]{:S(2)}, u32[]{:S(2)}) collective-permute-start(f32[64,128]{1,0:T(8,128)S(1)} %shard_map.65), channel_id=1, source_target_pairs={{0,16},{16,32},{32,48},{1,17},{17,33},{33,49},{2,18},{18,34},{34,5... | collective-permute-start | bytes 98312 | tf_op jit(solution)/shard_map/ppermute | solution.py:433
  54.1 18.6 %collective-permute-start.4 = (bf16[4,128,128]{2,1,0:T(8,128)(2,1)S(1)}, bf16[4,128,128]{2,1,0:T(8,128)(2,1)S(1)}, u32[]{:S(2)}, u32[]{:S(2)}) collective-permute-start(bf16[4,128,128]{2,1,0:T(8,128)(2,1)S(1)} %get-tuple-element.39), channel_id=1, source_target_pairs={{0,1},{1,0},{2,3},{3,2},{4,5},{5,4},{6,7},{7,6},{8,9},{9,8},{10,11... | collective-permute-start | bytes 393224 | tf_op jit(solution)/shard_map/ppermute | solution.py:439
  64.3 5.2 %copy-start = (f32[1024]{0:T(1024)S(1)}, f32[1024]{0:T(1024)}, u32[]{:S(2)}) copy-start(f32[1024]{0:T(1024)} %param.11) | copy-start | bytes 12292

commit v2 on v1

v2 whole, which is shorter than its diff:
```python
import jax
import jax.numpy as jnp
from jax import lax
from jax.experimental import pallas as pl
from jax.experimental.pallas import tpu as pltpu
from jax.sharding import Mesh
from jax.sharding import PartitionSpec as P

HEAD = 128
CHUNK = 256
GROUP = 16
CTX = ("x", "z", "c")
DP_CTX = ("dp", "x", "z", "c")
F32 = jnp.float32
BF16 = jnp.bfloat16


def one_if(flag):
    return jnp.where(flag, 1.0, 0.0)


def starts_of(lengths):
    rows = jnp.broadcast_to(lengths, (8, HEAD))
    before = one_if(
        lax.broadcasted_iota(jnp.int32, (HEAD, HEAD), 0) < lax.broadcasted_iota(jnp.int32, (HEAD, HEAD), 1)
    ).astype(BF16)
    high = jnp.dot((rows >> 8).astype(F32).astype(BF16), before, preferred_element_type=F32)
    low = jnp.dot((rows & 255).astype(F32).astype(BF16), before, preferred_element_type=F32)
    return high * 256.0 + low


def docs_of(positions, starts):
    below = one_if(starts[0:1] <= positions.astype(F32)).astype(BF16)
    return jnp.dot(below, jnp.ones((HEAD, HEAD), BF16), preferred_element_type=F32), below


def wide(rows):
    return jnp.concatenate([rows, rows], axis=1)


def fill_doc(first, starts, doc_s, m_s):
    count = m_s.shape[1]
    iota = lax.broadcasted_iota(jnp.int32, (count + 8, HEAD), 0)
    doc, below = docs_of(iota + (first - 8), starts)
    doc_s[...] = doc
    for j in (1, 2, 3):
        m_s[j - 1] = one_if(doc_s[8 - j : 8 - j + count] == doc_s[8:])
    return below


def conv(ext, taps, m_s, r0):
    acc = taps[0:1] * ext[8 + r0 : 8 + r0 + CHUNK]
    for j in (1, 2, 3):
        acc += taps[j : j + 1] * (ext[8 + r0 - j : 8 + r0 - j + CHUNK] * m_s[j - 1, r0 : r0 + CHUNK])
    return acc


def silu_of_half(half):
    return half * jnp.tanh(half) + half


def fill_live(doc, live_s):
    for r0 in range(0, live_s.shape[0], CHUNK):
        last = doc[8 + r0 + CHUNK - 1 : 8 + r0 + CHUNK]
        live_s[r0 : r0 + CHUNK] = one_if(doc[8 + r0 : 8 + r0 + CHUNK] == last).astype(BF16)


def kv_chunk(ext_k, ext_v, kw, vw, m_s, live_s, r0):
    key = silu_of_half(conv(ext_k, kw, m_s, r0)).astype(BF16)
    val = conv(ext_v, vw, m_s, r0).astype(BF16)
    live = live_s[r0 : r0 + CHUNK]
    tail = lax.dot_general(key * live, val, (((0,), (0,)), ((), ())), preferred_element_type=F32)
    return key, val, tail


def lanes(head, count=1):
    return pl.ds(pl.multiple_of(head * HEAD, HEAD), count * HEAD)


def run(copies):
    for copy in copies:
        copy.start()


def finish_all(copies):
    for copy in copies:
        copy.wait()


def late_kernel(
    here_ref, len_ref, k_hbm, v_hbm, w_ref,
    pk_hbm, val_hbm, st_ref, gate_ref, k0_ref, v0_ref,
    doc_s, m_s, live_s, ext_k, ext_v, kb, vb, pkb, valb, in_sem, out_sem, edge_sem,
    *, chips,
):
    rows = k_hbm.shape[0]
    chunks = rows // CHUNK
    pairs = kb.shape[0]
    tail_rows = pl.ds(CHUNK - GROUP, rows - CHUNK + GROUP)

    def fetch(p):
        cols = lanes(2 * p, 2)
        return [
            pltpu.make_async_copy(k_hbm.at[tail_rows, cols], kb.at[p], in_sem.at[0, p]),
            pltpu.make_async_copy(v_hbm.at[tail_rows, cols], vb.at[p], in_sem.at[1, p]),
        ]

    def store(p):
        two = pl.ds(2 * p, 2)
        return [
            pltpu.make_async_copy(pkb.at[two], pk_hbm.at[two], out_sem.at[0, p]),
            pltpu.make_async_copy(valb.at[two], val_hbm.at[two], out_sem.at[1, p]),
        ]

    edges = [
        pltpu.make_async_copy(k_hbm.at[pl.ds(0, CHUNK)], k0_ref, edge_sem.at[0]),
        pltpu.make_async_copy(v_hbm.at[pl.ds(0, CHUNK)], v0_ref, edge_sem.at[1]),
    ]
    for p in range(pairs):
        run(fetch(p))
    run(edges)

    here = here_ref[0]
    core = here % 2
    offset = here * rows
    starts = starts_of(len_ref[...])
    fill_doc(offset, starts, doc_s, m_s)
    fill_live(doc_s, live_s)
    chip = offset - core * rows
    first = (here // (2 * chips)) * (2 * chips * rows)
    mark = lax.broadcasted_iota(jnp.int32, (16, HEAD), 0)
    ends, _ = docs_of(first + mark * (2 * rows) - 1, starts)
    mine, _ = docs_of(chip + mark * rows - 1, starts)
    inner, _ = docs_of(offset + mark * CHUNK - 1, starts)
    keep_first = one_if(mine[1:2] == mine[0:1])
    keep_second = one_if(mine[2:3] == mine[1:2])
    second = jnp.full((1, HEAD), core, jnp.int32) == 1
    gate_ref[0:chips] = one_if(ends[1 : chips + 1] == ends[0:chips])
    one, zero = jnp.ones((1, HEAD), F32), jnp.zeros((1, HEAD), F32)
    rest = [
        jnp.where(second, one, keep_second),
        jnp.where(second, keep_second, one),
        jnp.where(second, keep_first, one),
        jnp.where(second, one, zero),
        jnp.where(second, one, keep_first),
        jnp.where(second, zero, one),
    ]
    for n, row in enumerate(rest):
        gate_ref[chips + n : chips + n + 1] = row
    for i in range(1, chunks):
        gate_ref[chips + 7 + i : chips + 8 + i] = one_if(inner[i : i + 1] == inner[0:1])
    for i in range(2, chunks + 1):
        gate_ref[chips + 9 + i : chips + 10 + i] = one_if(inner[i : i + 1] == inner[1:2])

    @pl.loop(0, pairs)
    def _(p):
        finish_all(fetch(p))
        for n in (0, 1):
            cols = slice(n * HEAD, (n + 1) * HEAD)
            ext_k[n, CHUNK - 8 :] = kb[p, :, cols].astype(F32)
            ext_v[n, CHUNK - 8 :] = vb[p, :, cols].astype(F32)
        taps = [(0.5 * w_ref[1, :, lanes(2 * p + n)], w_ref[2, :, lanes(2 * p + n)]) for n in (0, 1)]
        states = [jnp.zeros((HEAD, HEAD), F32)] * 2
        for i in range(1, chunks):
            r0 = i * CHUNK
            same = one_if(doc_s[8 + r0 - 1 : 8 + r0] == doc_s[8 + r0 + CHUNK - 1 : 8 + r0 + CHUNK])
            for n in (0, 1):
                key, val, tail = kv_chunk(ext_k.at[n], ext_v.at[n], *taps[n], m_s, live_s, r0)
                pkb[2 * p + n, r0 - CHUNK : r0] = key
                valb[2 * p + n, r0 - CHUNK : r0] = val
                states[n] = states[n] * same + tail
                st_ref[2 * p + n, i - 1] = states[n]
        run(store(p))

    finish_all(edges)
    for p in range(pairs):
        finish_all(store(p))


def first_kernel(
    here_ref, len_ref, gate_ref, k_ref, v_ref, rim_ref, w_ref, late_ref,
    pk_ref, val_ref, st_ref, tail_ref, doc_s, m_s, live_s, ext_k, ext_v,
    *, mine, rows, chips,
):
    heads = pk_ref.shape[0]
    here = here_ref[0]
    base = (here % 2 if mine else 1 - here % 2) * heads
    count = late_ref.shape[1] + 1
    fill_doc(here * rows, starts_of(len_ref[...]), doc_s, m_s)
    fill_live(doc_s, live_s)

    @pl.loop(0, heads // 2)
    def _(p):
        for n in (0, 1):
            cols = lanes(base + 2 * p + n)
            ext_k[n, 0:8] = rim_ref[1, :, cols].astype(F32)
            ext_v[n, 0:8] = rim_ref[2, :, cols].astype(F32)
            ext_k[n, 8:] = k_ref[:, cols].astype(F32)
            ext_v[n, 8:] = v_ref[:, cols].astype(F32)
        for n in (0, 1):
            h = 2 * p + n
            cols = lanes(base + h)
            key, val, tail = kv_chunk(
                ext_k.at[n], ext_v.at[n], 0.5 * w_ref[1, :, cols], w_ref[2, :, cols], m_s, live_s, 0
            )
            pk_ref[h] = key
            val_ref[h] = val
            st_ref[h, 0] = tail.astype(BF16)
            for i in range(1, count):
                state = late_ref[base + h, i - 1] + tail * gate_ref[chips + 10 + i : chips + 11 + i]
                if i < count - 1:
                    st_ref[h, i] = state.astype(BF16)
            tail_ref[h] = state.astype(BF16)


def attend_kernel(
    here_ref, len_ref, q_hbm, pkl_hbm, vall_hbm, pkf_ref, valf_ref, rim_ref, w_ref,
    pq_out, mix_out, doc_s, m_s, use_s, ext, allow_s, qb, kb, vb, in_sem, *staging,
    mine,
):
    heads, rows, _ = pq_out.shape
    chunks = rows // CHUNK
    pairs = heads // 2
    here = here_ref[0]
    base = (here % 2 if mine else 1 - here % 2) * heads
    pq_ref, mix_ref = staging[:2] if staging else (pq_out, mix_out)

    def fetch(p):
        two = pl.ds(base + 2 * p, 2)
        return [
            pltpu.make_async_copy(q_hbm.at[:, lanes(base + 2 * p, 2)], qb.at[p], in_sem.at[0, p]),
            pltpu.make_async_copy(pkl_hbm.at[two], kb.at[p], in_sem.at[1, p]),
            pltpu.make_async_copy(vall_hbm.at[two], vb.at[p], in_sem.at[2, p]),
        ]

    def store(p):
        two = pl.ds(2 * p, 2)
        return [
            pltpu.make_async_copy(pq_ref.at[two], pq_out.at[two], staging[2].at[0, p]),
            pltpu.make_async_copy(mix_ref.at[two], mix_out.at[two], staging[2].at[1, p]),
        ]

    for p in range(pairs):
        run(fetch(p))

    below = fill_doc(here * rows, starts_of(len_ref[...]), doc_s, m_s)
    across = lax.dot_general(
        jnp.ones((8, HEAD), BF16), below[8:], (((1,), (1,)), ((), ())), preferred_element_type=F32
    )
    causal = lax.broadcasted_iota(jnp.int32, (CHUNK, CHUNK), 1) <= lax.broadcasted_iota(
        jnp.int32, (CHUNK, CHUNK), 0
    )
    for i in range(chunks):
        r0 = i * CHUNK
        doc = doc_s[8 + r0 : 8 + r0 + CHUNK]
        same = wide(doc) == across[0:1, r0 : r0 + CHUNK]
        allow_s[i] = jnp.where(same & causal, 1.0, 0.0).astype(BF16)
        use_s[r0 : r0 + CHUNK] = one_if(doc == doc_s[8 + r0 - 1 : 8 + r0]).astype(BF16)

    @pl.loop(0, pairs)
    def _(p):
        finish_all(fetch(p))
        for n in (0, 1):
            ext[n, 0:8] = rim_ref[0, :, lanes(base + 2 * p + n)].astype(F32)
            ext[n, 8:] = qb[p, :, n * HEAD : (n + 1) * HEAD].astype(F32)
        taps = [0.5 * w_ref[0, :, lanes(base + 2 * p + n)] for n in (0, 1)]

        def make(i, n):
            rows = slice(i * CHUNK, (i + 1) * CHUNK)
            query = silu_of_half(conv(ext.at[n], taps[n], m_s, i * CHUNK)).astype(BF16)
            pq_ref[2 * p + n, rows] = query * use_s[rows]
            return query

        def mixed(i, n, query):
            r0 = i * CHUNK
            key = pkf_ref[2 * p + n] if i == 0 else kb[p, n, r0 - CHUNK : r0]
            val = valf_ref[2 * p + n] if i == 0 else vb[p, n, r0 - CHUNK : r0]
            scores = lax.dot_general(query, key, (((1,), (1,)), ((), ())), preferred_element_type=F32)
            weights = scores.astype(BF16) * allow_s[i]
            mix = jnp.dot(weights, val, preferred_element_type=F32)
            mix_ref[2 * p + n, r0 : r0 + CHUNK] = mix.astype(BF16)

        ahead = None
        for i in range(chunks):
            for n in (0, 1):
                query = make(i, n)
                if ahead is not None:
                    mixed(*ahead)
                ahead = (i, n, query)
        mixed(*ahead)
        if staging:
            run(store(p))

    if staging:
        for p in range(pairs):
            finish_all(store(p))


def finish_kernel(here_ref, gate_ref, pq_ref, mix_ref, st_ref, carried_ref, gain_ref, *rest, mine, chips):
    if mine:
        pqx_hbm, mixx_hbm, out_hbm, pqx_ref, mixx_ref, outb, out_sem, next_sem = rest
        onward = [
            pltpu.make_async_copy(pqx_hbm, pqx_ref, next_sem.at[0]),
            pltpu.make_async_copy(mixx_hbm, mixx_ref, next_sem.at[1]),
        ]
    else:
        _, out_hbm, outb, out_sem = rest
        onward = []
    heads, rows, _ = pq_ref.shape
    chunks = rows // CHUNK
    base = (here_ref[0] % 2 if mine else 1 - here_ref[0] % 2) * heads
    mean = jnp.full((HEAD, HEAD), 1.0 / HEAD, BF16)
    run(onward)

    def store(p, i):
        rows = pl.ds(i * CHUNK, CHUNK)
        return pltpu.make_async_copy(
            outb.at[p, rows], out_hbm.at[rows, lanes(base + 2 * p, 2)], out_sem.at[p, i]
        )

    @pl.loop(0, heads // 2)
    def _(p):
        gain = [gain_ref[:, lanes(base + 2 * p + n)] for n in (0, 1)]

        def blend(i, n):
            h = 2 * p + n
            state = carried_ref[h].astype(F32)
            if i:
                state = st_ref[h, i - 1].astype(F32) + state * gate_ref[chips + 7 + i : chips + 8 + i]
            rows = slice(i * CHUNK, (i + 1) * CHUNK)
            held = jnp.dot(pq_ref[h, rows], state.astype(BF16), preferred_element_type=F32)
            return mix_ref[h, rows].astype(F32) + held

        def norm(i, n, mixture):
            square = jnp.dot((mixture * mixture).astype(BF16), mean, preferred_element_type=F32)
            scale = lax.rsqrt(square + 1e-06) * gain[n]
            outb[p, i * CHUNK : (i + 1) * CHUNK, n * HEAD : (n + 1) * HEAD] = (mixture * scale).astype(BF16)
            if n:
                store(p, i).start()

        ahead = None
        for i in range(chunks):
            for n in (0, 1):
                mixture = blend(i, n)
                if ahead is not None:
                    norm(*ahead)
                ahead = (i, n, mixture)
        norm(*ahead)

    finish_all(onward)
    for p in range(heads // 2):
        for i in range(chunks):
            store(p, i).wait()


def rim_kernel(q_ref, k_ref, v_ref, out_ref):
    out_ref[0] = q_ref[...]
    out_ref[1] = k_ref[...]
    out_ref[2] = v_ref[...]


def join_kernel(gate_ref, own_ref, got_ref, out_ref, *, chips):
    own, got = gate_ref[chips : chips + 1], gate_ref[chips + 1 : chips + 2]
    out_ref[...] = (own_ref[...].astype(F32) * own + got_ref[...].astype(F32) * got).astype(BF16)


def total_kernel(gate_ref, spread_ref, out_ref):
    total = jnp.zeros(out_ref.shape, F32)
    for z in range(spread_ref.shape[0]):
        total = total * gate_ref[z : z + 1] + spread_ref[z].astype(F32)
    out_ref[...] = total


def enter_kernel(gate_ref, spread_ref, near_ref, far_ref, out_ref):
    running = near_ref[...] + far_ref[...]
    for z in range(spread_ref.shape[0]):
        out_ref[z] = running.astype(BF16)
        running = running * gate_ref[z : z + 1] + spread_ref[z].astype(F32)


def carry_kernel(gate_ref, entered_ref, own_ref, got_ref, mine_ref, other_ref, *, chips):
    gate = [gate_ref[chips + 2 + n : chips + 3 + n] for n in range(4)]
    entered = entered_ref[...].astype(F32)
    mine_ref[...] = (entered * gate[0] + got_ref[...].astype(F32) * gate[1]).astype(BF16)
    other_ref[...] = (entered * gate[2] + own_ref[...].astype(F32) * gate[3]).astype(BF16)


def in_hbm(x):
    return pltpu.with_memory_space_constraint(x, pltpu.HBM)


def params(mib):
    return pltpu.CompilerParams(vmem_limit_bytes=mib * 1024 * 1024)


def small(kernel, outs, *args):
    return pl.pallas_call(
        kernel, out_shape=outs, compiler_params=pltpu.CompilerParams(vmem_limit_bytes=4 * 1024 * 1024)
    )(*args)


def shaped(*shape, dtype=BF16):
    return jax.ShapeDtypeStruct(shape, dtype)


def per_device(query_rows, key_rows, value_rows, lengths, conv_weight, out_gain):
    query_rows, key_rows, value_rows = (in_hbm(x) for x in (query_rows, key_rows, value_rows))
    rows, channels = query_rows.shape
    heads = channels // HEAD
    half = heads // 2
    chunks = rows // CHUNK
    chips, x_count = lax.axis_size("z"), lax.axis_size("x")
    ctx_count = x_count * chips * 2
    here = lax.axis_index(CTX).astype(jnp.int32).reshape(1)
    swap = [(0, 1), (1, 0)]

    smem = pl.BlockSpec(memory_space=pltpu.SMEM)
    last_rows = pl.BlockSpec((8, channels), lambda i: (rows // 8 - 1, 0))
    rims = pl.pallas_call(
        rim_kernel,
        grid=(1,),
        in_specs=[last_rows] * 3,
        out_specs=pl.BlockSpec((3, 8, channels), lambda i: (0, 0, 0)),
        out_shape=shaped(3, 8, channels),
        compiler_params=params(4),
        name="rim",
    )(query_rows, key_rows, value_rows)
    rims = lax.ppermute(rims, CTX, [(i, i + 1) for i in range(ctx_count - 1)])

    vmem = pl.BlockSpec(memory_space=pltpu.VMEM)
    hbm = pl.BlockSpec(memory_space=pl.ANY)
    lengths = lengths.reshape(1, -1)
    gains = out_gain.reshape(1, -1)
    gate_rows = 24
    pairs, half_pairs = heads // 2, half // 2
    later = rows - CHUNK
    dma = lambda *shape: pltpu.SemaphoreType.DMA(shape)

    def masks(count):
        return [
            pltpu.VMEM((count + 8, HEAD), F32),
            pltpu.VMEM((3, count, HEAD), F32),
            pltpu.VMEM((count, HEAD), BF16),
        ]

    pk_late, val_late, st_late, gates, key_head, value_head = pl.pallas_call(
        lambda *refs: late_kernel(*refs, chips=chips),
        in_specs=[smem, vmem, hbm, hbm, vmem],
        out_specs=[hbm, hbm, vmem, vmem, vmem, vmem],
        out_shape=[
            pltpu.HBM((heads, later, HEAD), BF16),
            pltpu.HBM((heads, later, HEAD), BF16),
            shaped(heads, chunks - 1, HEAD, HEAD, dtype=F32),
            shaped(gate_rows, HEAD, dtype=F32),
            shaped(CHUNK, channels),
            shaped(CHUNK, channels),
        ],
        scratch_shapes=masks(rows)
        + [pltpu.VMEM((2, rows + 8, HEAD), F32)] * 2
        + [pltpu.VMEM((pairs, later + GROUP, 2 * HEAD), BF16)] * 2
        + [pltpu.VMEM((heads, later, HEAD), BF16)] * 2
        + [dma(2, pairs), dma(2, pairs), dma(2)],
        compiler_params=params(20),
        name="late",
    )(here, lengths, key_rows, value_rows, conv_weight)
    pk_late, val_late = in_hbm(pk_late), in_hbm(val_late)

    def first(mine):
        return pl.pallas_call(
            lambda *refs: first_kernel(*refs, mine=mine, rows=rows, chips=chips),
            in_specs=[smem] + [vmem] * 7,
            out_specs=[vmem] * 4,
            out_shape=[
                shaped(half, CHUNK, HEAD),
                shaped(half, CHUNK, HEAD),
                shaped(half, chunks - 1, HEAD, HEAD),
                shaped(half, HEAD, HEAD),
            ],
            scratch_shapes=masks(CHUNK) + [pltpu.VMEM((2, CHUNK + 8, HEAD), F32)] * 2,
            compiler_params=params(8),
            name="first",
        )(here, lengths, gates, key_head, value_head, rims, conv_weight, st_late)

    pk_other, val_other, inner_other, other = first(False)
    got = lax.ppermute(other, "c", swap)
    pk_own, val_own, inner_own, own = first(True)

    state = (half, HEAD, HEAD)
    chip_tail = small(lambda *r: join_kernel(*r, chips=chips), pltpu.HBM(state, BF16), gates, own, got)
    spread = lax.all_to_all(chip_tail.reshape(chips, -1, HEAD), "z", 0, 0, tiled=True)

    def attend(mine, pk_first, val_first):
        shape = (half, rows, HEAD)
        return pl.pallas_call(
            lambda *refs: attend_kernel(*refs, mine=mine),
            in_specs=[smem, vmem, hbm, hbm, hbm, vmem, vmem, vmem, vmem],
            out_specs=[vmem if mine else hbm] * 2,
            out_shape=[shaped(*shape) if mine else pltpu.HBM(shape, BF16)] * 2,
            scratch_shapes=masks(rows)
            + [pltpu.VMEM((2, rows + 8, HEAD), F32), pltpu.VMEM((chunks, CHUNK, CHUNK), BF16)]
            + [pltpu.VMEM((half_pairs, rows, 2 * HEAD), BF16)]
            + [pltpu.VMEM((half_pairs, 2, later, HEAD), BF16)] * 2
            + [dma(3, half_pairs)]
            + ([] if mine else [pltpu.VMEM(shape, BF16)] * 2 + [dma(2, half_pairs)]),
            compiler_params=params(24),
            name="attend",
        )(here, lengths, query_rows, pk_late, val_late, pk_first, val_first, rims, conv_weight)

    phi_other, mix_other = (in_hbm(x) for x in attend(False, pk_other, val_other))
    phi_own, mix_own = attend(True, pk_own, val_own)

    row_total = small(total_kernel, shaped(*spread.shape[1:], dtype=F32), gates, spread)
    far = lax.ppermute(row_total, "x", [(1, 3)])
    near = lax.ppermute(row_total, "x", [(i, i + 1) for i in range(x_count - 1)])
    entering = small(enter_kernel, pltpu.HBM(spread.shape, BF16), gates, spread, near, far)
    entered = lax.all_to_all(entering, "z", 0, 0, tiled=True).reshape(state)
    carried_own, carried_other = small(
        lambda *r: carry_kernel(*r, chips=chips), [shaped(*state)] * 2, gates, entered, own, got
    )
    carried_far = lax.ppermute(carried_other, "c", swap)

    def finish(mine, phi, mix, inner, carried, *others):
        shape = (half, rows, HEAD)
        ahead = [shaped(*shape)] * 2 if mine else []
        args = (here, gates, phi, mix, inner, carried, gains, *others)
        return pl.pallas_call(
            lambda *refs: finish_kernel(*refs, mine=mine, chips=chips),
            in_specs=[smem] + [vmem] * 6 + [hbm] * len(others),
            out_specs=[hbm] + [vmem] * len(ahead),
            out_shape=[pltpu.HBM((rows, channels), BF16)] + ahead,
            scratch_shapes=[pltpu.VMEM((half_pairs, rows, 2 * HEAD), BF16), dma(half_pairs, chunks)]
            + ([dma(2)] if mine else []),
            input_output_aliases={} if mine else {len(args) - 1: 0},
            compiler_params=params(12),
            name="finish",
        )(*args)

    done, phi_other, mix_other = finish(
        True, phi_own, mix_own, inner_own, carried_own, phi_other, mix_other
    )
    return finish(False, phi_other, mix_other, inner_other, carried_far, done)[0]


def solution(mesh):
    finer = Mesh(mesh.devices.reshape(mesh.shape["dp"], 4, 8, 2), DP_CTX)

    return jax.shard_map(
        per_device,
        mesh=finer,
        in_specs=(P(DP_CTX, None), P(DP_CTX, None), P(DP_CTX, None), P("dp"), P(), P()),
        out_specs=P(DP_CTX, None),
        check_vma=False,
    )
```

time: 76.5 us -> 67 us (0.88)
  the two profiles are of different devices: /device:TPU:3 before, /device:TPU:27 now
where the time goes in v2:
time: 67 us; the launch traced here: 66.5 us
  blocking collectives  26.3 us (39%)
  Pallas kernels  22.5 us (34%)
  starting transfers between devices  14.7 us (22%)
  waiting for transfers between devices  2.83 us (4%)
    all_to_all x1, blocking collectives, per_device(): lax.all_to_all(chip_tail.reshape(chips, -1, HEAD), 'z', 0, 0, tiled=True)  15.1 us
    all_to_all x1, blocking collectives, per_device(): entered = lax.all_to_all(entering, 'z', 0, 0, tiled=True).reshape(state)  11.2 us
    pallas_call x2, Pallas kernels, attend(): pl.pallas_call(lambda *refs: attend_kernel(*refs, mine=mine), in_specs=[s...  7.96 us
    pallas_call x1, Pallas kernels, per_device(): pl.pallas_call(lambda *refs: late_kernel(*refs, chips=chips), in_specs=[s...  6.16 us
    ppermute x1, starting transfers between devices, per_device(): carried_far = lax.ppermute(carried_other, 'c', swap)  4.84 us
    ppermute x1, starting transfers between devices, per_device(): rims = lax.ppermute(rims, CTX, [(i, i + 1) for i in range(ctx_count - 1)])  4.09 us
    ppermute x1, starting transfers between devices, per_device(): far = lax.ppermute(row_total, 'x', [(1, 3)])  3.75 us
    pallas_call x2, Pallas kernels, finish(): pl.pallas_call(lambda *refs: finish_kernel(*refs, mine=mine, chips=chips)...  3.66 us
  transfers between devices with their start and end apart: 5, of which 2 were waited for; matrix products, arithmetic and copies ran while one was open for 0% of the time, Pallas kernels for 26%

profile of v2, /device:TPU:27, one launch (start us, length us, event | category | flops | bytes accessed | tf_op | source)
XLA Modules:
  0.0 66.5 jit_solution(155983455207838924)
XLA Ops:
  0.0 0.0 copy-start
  0.0 0.0 copy-start.2
  0.0 0.8 %rim.1 = bf16[3,8,1024]{2,1,0:T(8,128)(2,1)S(1)} custom-call(bf16[1024,1024]{1,0:T(8,128)(2,1)} %refs_2_.5, bf16[1024,1024]{1,0:T(8,128)(2,1)} %k_ref.1, bf16[1024,1024]{1,0:T(8,128)(2,1)} %v_ref.1), custom_call_target="tpu_custom_call" | custom-call | tf_op jit(solution)/shard_map/rim/pallas_call | solution.py:419
  0.8 4.1 %collective-permute-start = (bf16[3,8,1024]{2,1,0:T(8,128)(2,1)S(1)}, bf16[3,8,1024]{2,1,0:T(8,128)(2,1)S(1)}, u32[]{:S(2)}, u32[]{:S(2)}) collective-permute-start(bf16[3,8,1024]{2,1,0:T(8,128)(2,1)S(1)} %rim.1), channel_id=1, source_target_pairs={{0,1},{1,2},{2,3},{3,4},{4,5},{5,6},{6,7},{7,8},{8,9},{9,10},{10,1... | collective-permute-start | bytes 147464 | tf_op jit(solution)/shard_map/ppermute | solution.py:428
  4.9 0.0 copy-done
  4.9 0.0 copy-done.2
  4.9 6.2 %late.1 = (bf16[8,768,128]{2,1,0:T(8,128)(2,1)}, bf16[8,768,128]{2,1,0:T(8,128)(2,1)}, f32[8,3,128,128]{3,2,1,0:T(8,128)S(1)}, f32[24,128]{1,0:T(8,128)S(1)}, bf...) custom-call(s32[1]{0:T(128)} %bitcast.refs_0_, s32[1,128]{1,0:T(1,128)S(1)} %bitcast.8, ...), custom_call_target="tpu_custom_call" | custom-call | tf_op jit(solution)/shard_map/late/pallas_call | solution.py:446
  11.1 0.0 collective-permute-done.refs_5_.refs_7_
  11.1 1.2 %first.3 = (bf16[4,256,128]{2,1,0:T(8,128)(2,1)S(1)}, bf16[4,256,128]{2,1,0:T(8,128)(2,1)S(1)}, bf16[4,3,128,128]{3,2,1,0:T(8,128)(2,1)S(1)}, bf16[4,128,128]{2,1,0:T(8,128)(2,1)S(1)}) custom-call(s32[1]{0:T(128)} %bitcast.refs_0_, s32[1,128]{1,0:T(1,128)S(1)} %bitcast.9, f32[24,128]{1,0:T(8,128)S(1)} %get-tuple-element.28.refs_2_.r_0_.gate_ref.refs_1_, ...), custom_call_target="tpu_custom_call" | custom-call | tf_op jit(solution)/shard_map/first/pallas_call | solution.py:469
  12.3 0.1 collective-permute-start.1
  12.4 1.2 %first.2 = (bf16[4,256,128]{2,1,0:T(8,128)(2,1)S(1)}, bf16[4,256,128]{2,1,0:T(8,128)(2,1)S(1)}, bf16[4,3,128,128]{3,2,1,0:T(8,128)(2,1)S(1)}, bf16[4,128,128]{2,1,0:T(8,128)(2,1)S(1)}) custom-call(s32[1]{0:T(128)} %bitcast.refs_0_, s32[1,128]{1,0:T(1,128)S(1)} %bitcast.10, f32[24,128]{1,0:T(8,128)S(1)} %get-tuple-element.28.refs_2_.r_0_.gate_ref.refs_1_, ...), custom_call_target="tpu_custom_call" | custom-call | tf_op jit(solution)/shard_map/first/pallas_call | solution.py:469
  13.6 0.1 collective-permute-done.1.r_2_.r_3_
  13.7 0.7 %shard_map.64 = bf16[4,128,128]{2,1,0:T(8,128)(2,1)} custom-call(f32[24,128]{1,0:T(8,128)S(1)} %get-tuple-element.28.refs_2_.r_0_.gate_ref.refs_1_, bf16[4,128,128]{2,1,0:T(8,128)(2,1)S(1)} %get-tuple-element.39.r_1_.r_2_, bf16[4,128,128]{2,1,0:T(8,128)(2,1)S(1)} %collective-permute-done.1.r_2_.r_3_), custom_call_target="tpu_custom_call" | custom-call | tf_op jit(solution)/shard_map/pallas_call | solution.py:397
  14.4 15.1 %all_to_all.10.spread_ref = bf16[8,64,128]{2,1,0:T(8,128)(2,1)S(1)} all-to-all(bf16[8,64,128]{2,1,0:T(8,128)(2,1)} %bitcast.13), channel_id=1, replica_groups=mesh['dp'=4,'x'=4,'z'=8,'c'=2] {'z'}, dimensions={0} | all-to-all | bytes 262144 | tf_op jit(solution)/shard_map/all_to_all | solution.py:490
  29.6 3.8 %collective-permute-start.3 = (f32[64,128]{1,0:T(8,128)S(1)}, f32[64,128]{1,0:T(8,128)S(1)}, u32[]{:S(2)}, u32[]{:S(2)}) collective-permute-start(f32[64,128]{1,0:T(8,128)S(1)} %shard_map.65), channel_id=1, source_target_pairs={{16,48},{17,49},{18,50},{19,51},{20,52},{21,53},{22,54},{23,55},{2... | collective-permute-start | bytes 98312 | tf_op jit(solution)/shard_map/ppermute | solution.py:513
  33.4 1.9 %collective-permute-start.2 = (f32[64,128]{1,0:T(8,128)S(1)}, f32[64,128]{1,0:T(8,128)S(1)}, u32[]{:S(2)}, u32[]{:S(2)}) collective-permute-start(f32[64,128]{1,0:T(8,128)S(1)} %shard_map.65), channel_id=1, source_target_pairs={{0,16},{16,32},{32,48},{1,17},{17,33},{33,49},{2,18},{18,34},{34,5... | collective-permute-start | bytes 98312 | tf_op jit(solution)/shard_map/ppermute | solution.py:514
  35.3 0.0 collective-permute-done.3.far_ref
  35.3 2.7 %collective-permute-done.2.near_ref = f32[64,128]{1,0:T(8,128)S(1)} collective-permute-done((f32[64,128]{1,0:T(8,128)S(1)}, f32[64,128]{1,0:T(8,128)S(1)}, u32[]{:S(2)}, u32[]{:S(2)}) %collective-permute-start.2) | collective-permute-done | bytes 32800 | tf_op jit(solution)/shard_map/ppermute | solution.py:514
  38.0 0.7 %shard_map.66 = bf16[8,64,128]{2,1,0:T(8,128)(2,1)} custom-call(f32[24,128]{1,0:T(8,128)S(1)} %get-tuple-element.28.refs_2_.r_0_.gate_ref.refs_1_, bf16[8,64,128]{2,1,0:T(8,128)(2,1)S(1)} %all_to_all.10.spread_ref, f32[64,128]{1,0:T(8,128)S(1)} %collective-permute-done.2.near_ref, f32[64,128]{1,0:T(8,128)S(1)} %collective-permute-done.3.far_ref), custom_call_target="tpu_custom_call" | custom-call | tf_op jit(solution)/shard_map/pallas_call | solution.py:397
  38.7 11.2 %all_to_all.11 = bf16[8,64,128]{2,1,0:T(8,128)(2,1)S(1)} all-to-all(bf16[8,64,128]{2,1,0:T(8,128)(2,1)} %shard_map.66), channel_id=1, replica_groups=mesh['dp'=4,'x'=4,'z'=8,'c'=2] {'z'}, dimensions={0} | all-to-all | bytes 262144 | tf_op jit(solution)/shard_map/all_to_all | solution.py:516
  49.9 0.1 shard_map.67
  50.0 4.8 %collective-permute-start.4 = (bf16[4,128,128]{2,1,0:T(8,128)(2,1)S(1)}, bf16[4,128,128]{2,1,0:T(8,128)(2,1)S(1)}, u32[]{:S(2)}, u32[]{:S(2)}) collective-permute-start(bf16[4,128,128]{2,1,0:T(8,128)(2,1)S(1)} %get-tuple-element.49), channel_id=1, source_target_pairs={{0,1},{1,0},{2,3},{3,2},{4,5},{5,4},{6,7},{7,6},{8,9},{9,8},{10,11... | collective-permute-start | bytes 393224 | tf_op jit(solution)/shard_map/ppermute | solution.py:520
  54.8 3.6 %attend.2 = (bf16[4,1024,128]{2,1,0:T(8,128)(2,1)S(1)}, bf16[4,1024,128]{2,1,0:T(8,128)(2,1)S(1)}) custom-call(s32[1]{0:T(128)} %bitcast.refs_0_, s32[1,128]{1,0:T(1,128)S(1)} %bitcast.11, bf16[1024,1024]{1,0:T(8,128)(2,1)} %refs_2_.5, bf16[8,768,128]{2,1,0:T(8,128)(2,1)} %get-tuple-element.29.refs_3_, bf16[8,768,128]{2,1,0:T(8,128)(2,1)} %get-tuple-element.30.refs_4_, ...), custom_call_target="tpu_custom_call" | custom-call | tf_op jit(solution)/shard_map/attend/pallas_call | solution.py:494
  58.4 0.0 copy-start.1
  58.4 4.4 %attend.3 = (bf16[4,1024,128]{2,1,0:T(8,128)(2,1)}, bf16[4,1024,128]{2,1,0:T(8,128)(2,1)}) custom-call(s32[1]{0:T(128)} %bitcast.refs_0_, s32[1,128]{1,0:T(1,128)S(1)} %bitcast.12, bf16[1024,1024]{1,0:T(8,128)(2,1)} %refs_2_.5, bf16[8,768,128]{2,1,0:T(8,128)(2,1)} %get-tuple-element.29.refs_3_, bf16[8,768,128]{2,1,0:T(8,128)(2,1)} %get-tuple-element.30.refs_4_, ...), custom_call_target="tpu_custom_call" | custom-call | tf_op jit(solution)/shard_map/attend/pallas_call | solution.py:494
  62.8 0.0 copy-done.1
  62.8 1.8 %finish.2 = (bf16[1024,1024]{1,0:T(8,128)(2,1)}, bf16[4,1024,128]{2,1,0:T(8,128)(2,1)S(1)}, bf16[4,1024,128]{2,1,0:T(8,128)(2,1)S(1)}) custom-call(s32[1]{0:T(128)} %bitcast.refs_0_, f32[24,128]{1,0:T(8,128)S(1)} %get-tuple-element.28.refs_2_.r_0_.gate_ref.refs_1_, bf16[4,1024,128]{2,1,0:T(8,128)(2,1)S(1)} %get-tuple-element.36.refs_2_, ...), custom_call_target="tpu_custom_call" | custom-call | tf_op jit(solution)/shard_map/finish/pallas_call | solution.py:526
  64.7 0.0 collective-permute-done.4.refs_5_
  64.7 1.8 %finish.3 = bf16[1024,1024]{1,0:T(8,128)(2,1)} custom-call(s32[1]{0:T(128)} %bitcast.refs_0_, f32[24,128]{1,0:T(8,128)S(1)} %get-tuple-element.28.refs_2_.r_0_.gate_ref.refs_1_, bf16[4,1024,128]{2,1,0:T(8,128)(2,1)S(1)} %get-tuple-element.46.refs_2_, bf16[4,1024,128]{2,1,0:T(8,128)(2,1)S(1)} %get-tuple-element.47.refs_3_, ...), custom_call_target="tpu_custom_call", output_to_operand_aliasing={{}: (7, {})} | custom-call | tf_op jit(solution)/shard_map/finish/pallas_call | solution.py:526
  (1 shorter events, 0.0 us)
Async XLA Ops:
  0.0 4.9 %copy-start = (f32[3,4,1024]{2,1,0:T(4,128)S(1)}, f32[3,4,1024]{2,1,0:T(4,128)}, u32[]{:S(2)}) copy-start(f32[3,4,1024]{2,1,0:T(4,128)} %refs_8_.3) | copy-start | bytes 147460
  0.0 4.9 %copy-start.2 = (s32[128]{0:T(128)S(1)}, s32[128]{0:T(128)}, u32[]{:S(2)}) copy-start(s32[128]{0:T(128)} %param.9) | copy-start | bytes 1540
  0.8 10.3 %collective-permute-start = (bf16[3,8,1024]{2,1,0:T(8,128)(2,1)S(1)}, bf16[3,8,1024]{2,1,0:T(8,128)(2,1)S(1)}, u32[]{:S(2)}, u32[]{:S(2)}) collective-permute-start(bf16[3,8,1024]{2,1,0:T(8,128)(2,1)S(1)} %rim.1), channel_id=1, source_target_pairs={{0,1},{1,2},{2,3},{3,4},{4,5},{5,6},{6,7},{7,8},{8,9},{9,10},{10,1... | collective-permute-start | bytes 147464 | tf_op jit(solution)/shard_map/ppermute | solution.py:428
  12.3 1.4 %collective-permute-start.1 = (bf16[4,128,128]{2,1,0:T(8,128)(2,1)S(1)}, bf16[4,128,128]{2,1,0:T(8,128)(2,1)S(1)}, u32[]{:S(2)}, u32[]{:S(2)}) collective-permute-start(bf16[4,128,128]{2,1,0:T(8,128)(2,1)S(1)} %get-tuple-element.40), channel_id=1, source_target_pairs={{0,1},{1,0},{2,3},{3,2},{4,5},{5,4},{6,7},{7,6},{8,9},{9,8},{10,11... | collective-permute-start | bytes 393224 | tf_op jit(solution)/shard_map/ppermute | solution.py:485
  29.6 5.7 %collective-permute-start.3 = (f32[64,128]{1,0:T(8,128)S(1)}, f32[64,128]{1,0:T(8,128)S(1)}, u32[]{:S(2)}, u32[]{:S(2)}) collective-permute-start(f32[64,128]{1,0:T(8,128)S(1)} %shard_map.65), channel_id=1, source_target_pairs={{16,48},{17,49},{18,50},{19,51},{20,52},{21,53},{22,54},{23,55},{2... | collective-permute-start | bytes 98312 | tf_op jit(solution)/shard_map/ppermute | solution.py:513
  33.4 4.7 %collective-permute-start.2 = (f32[64,128]{1,0:T(8,128)S(1)}, f32[64,128]{1,0:T(8,128)S(1)}, u32[]{:S(2)}, u32[]{:S(2)}) collective-permute-start(f32[64,128]{1,0:T(8,128)S(1)} %shard_map.65), channel_id=1, source_target_pairs={{0,16},{16,32},{32,48},{1,17},{17,33},{33,49},{2,18},{18,34},{34,5... | collective-permute-start | bytes 98312 | tf_op jit(solution)/shard_map/ppermute | solution.py:514
  50.0 14.7 %collective-permute-start.4 = (bf16[4,128,128]{2,1,0:T(8,128)(2,1)S(1)}, bf16[4,128,128]{2,1,0:T(8,128)(2,1)S(1)}, u32[]{:S(2)}, u32[]{:S(2)}) collective-permute-start(bf16[4,128,128]{2,1,0:T(8,128)(2,1)S(1)} %get-tuple-element.49), channel_id=1, source_target_pairs={{0,1},{1,0},{2,3},{3,2},{4,5},{5,4},{6,7},{7,6},{8,9},{9,8},{10,11... | collective-permute-start | bytes 393224 | tf_op jit(solution)/shard_map/ppermute | solution.py:520
  58.4 4.4 %copy-start.1 = (f32[1024]{0:T(1024)S(1)}, f32[1024]{0:T(1024)}, u32[]{:S(2)}) copy-start(f32[1024]{0:T(1024)} %param.11) | copy-start | bytes 12292

commit v3 on v2

--- a/solution.py
+++ b/solution.py
@@ -127,9 +127,9 @@
     fill_doc(offset, starts, doc_s, m_s)
     fill_live(doc_s, live_s)
     chip = offset - core * rows
-    first = (here // (2 * chips)) * (2 * chips * rows)
+    chip_mark = lax.broadcasted_iota(jnp.int32, (chips + 8, HEAD), 0)
     mark = lax.broadcasted_iota(jnp.int32, (16, HEAD), 0)
-    ends, _ = docs_of(first + mark * (2 * rows) - 1, starts)
+    ends, _ = docs_of(chip_mark * (2 * rows) - 1, starts)
     mine, _ = docs_of(chip + mark * rows - 1, starts)
     inner, _ = docs_of(offset + mark * CHUNK - 1, starts)
     keep_first = one_if(mine[1:2] == mine[0:1])
@@ -223,7 +223,16 @@
     pairs = heads // 2
     here = here_ref[0]
     base = (here % 2 if mine else 1 - here % 2) * heads
-    pq_ref, mix_ref = staging[:2] if staging else (pq_out, mix_out)
+    if mine:
+        kf_s, vf_s, first_sem = staging
+        firsts = [
+            pltpu.make_async_copy(pkf_ref, kf_s, first_sem.at[0]),
+            pltpu.make_async_copy(valf_ref, vf_s, first_sem.at[1]),
+        ]
+        pq_ref, mix_ref, pkf_ref, valf_ref = pq_out, mix_out, kf_s, vf_s
+    else:
+        firsts = []
+        pq_ref, mix_ref, out_sem = staging
 
     def fetch(p):
         two = pl.ds(base + 2 * p, 2)
@@ -236,10 +245,11 @@
     def store(p):
         two = pl.ds(2 * p, 2)
         return [
-            pltpu.make_async_copy(pq_ref.at[two], pq_out.at[two], staging[2].at[0, p]),
-            pltpu.make_async_copy(mix_ref.at[two], mix_out.at[two], staging[2].at[1, p]),
-        ]
-
+            pltpu.make_async_copy(pq_ref.at[two], pq_out.at[two], out_sem.at[0, p]),
+            pltpu.make_async_copy(mix_ref.at[two], mix_out.at[two], out_sem.at[1, p]),
+        ]
+
+    run(firsts)
     for p in range(pairs):
         run(fetch(p))
 
@@ -256,6 +266,7 @@
         same = wide(doc) == across[0:1, r0 : r0 + CHUNK]
         allow_s[i] = jnp.where(same & causal, 1.0, 0.0).astype(BF16)
         use_s[r0 : r0 + CHUNK] = one_if(doc == doc_s[8 + r0 - 1 : 8 + r0]).astype(BF16)
+    finish_all(firsts)
 
     @pl.loop(0, pairs)
     def _(p):
@@ -288,10 +299,10 @@
                     mixed(*ahead)
                 ahead = (i, n, query)
         mixed(*ahead)
-        if staging:
+        if not mine:
             run(store(p))
 
-    if staging:
+    if not mine:
         for p in range(pairs):
             finish_all(store(p))
 
@@ -364,18 +375,11 @@
     out_ref[...] = (own_ref[...].astype(F32) * own + got_ref[...].astype(F32) * got).astype(BF16)
 
 
-def total_kernel(gate_ref, spread_ref, out_ref):
-    total = jnp.zeros(out_ref.shape, F32)
-    for z in range(spread_ref.shape[0]):
-        total = total * gate_ref[z : z + 1] + spread_ref[z].astype(F32)
-    out_ref[...] = total
-
-
-def enter_kernel(gate_ref, spread_ref, near_ref, far_ref, out_ref):
-    running = near_ref[...] + far_ref[...]
-    for z in range(spread_ref.shape[0]):
-        out_ref[z] = running.astype(BF16)
-        running = running * gate_ref[z : z + 1] + spread_ref[z].astype(F32)
+def enter_kernel(gate_ref, spread_ref, out_ref):
+    running = jnp.zeros(spread_ref.shape[1:], F32)
+    for n in range(spread_ref.shape[0]):
+        out_ref[n] = running.astype(BF16)
+        running = running * gate_ref[n : n + 1] + spread_ref[n].astype(F32)
 
 
 def carry_kernel(gate_ref, entered_ref, own_ref, got_ref, mine_ref, other_ref, *, chips):
@@ -409,8 +413,8 @@
     heads = channels // HEAD
     half = heads // 2
     chunks = rows // CHUNK
-    chips, x_count = lax.axis_size("z"), lax.axis_size("x")
-    ctx_count = x_count * chips * 2
+    chips = lax.axis_size("x") * lax.axis_size("z")
+    ctx_count = 2 * chips
     here = lax.axis_index(CTX).astype(jnp.int32).reshape(1)
     swap = [(0, 1), (1, 0)]
 
@@ -425,13 +429,13 @@
         compiler_params=params(4),
         name="rim",
     )(query_rows, key_rows, value_rows)
-    rims = lax.ppermute(rims, CTX, [(i, i + 1) for i in range(ctx_count - 1)])
+    rims = lax.ppermute(rims, CTX, [(i, (i + 1) % ctx_count) for i in range(ctx_count)])
 
     vmem = pl.BlockSpec(memory_space=pltpu.VMEM)
     hbm = pl.BlockSpec(memory_space=pl.ANY)
     lengths = lengths.reshape(1, -1)
     gains = out_gain.reshape(1, -1)
-    gate_rows = 24
+    gate_rows = chips + 16
     pairs, half_pairs = heads // 2, half // 2
     later = rows - CHUNK
     dma = lambda *shape: pltpu.SemaphoreType.DMA(shape)
@@ -486,14 +490,14 @@
     pk_own, val_own, inner_own, own = first(True)
 
     state = (half, HEAD, HEAD)
-    chip_tail = small(lambda *r: join_kernel(*r, chips=chips), pltpu.HBM(state, BF16), gates, own, got)
-    spread = lax.all_to_all(chip_tail.reshape(chips, -1, HEAD), "z", 0, 0, tiled=True)
+    chip_tail = small(lambda *r: join_kernel(*r, chips=chips), shaped(*state), gates, own, got)
+    spread = lax.all_to_all(chip_tail.reshape(chips, -1, HEAD), ("x", "z"), 0, 0, tiled=True)
 
     def attend(mine, pk_first, val_first):
         shape = (half, rows, HEAD)
         return pl.pallas_call(
             lambda *refs: attend_kernel(*refs, mine=mine),
-            in_specs=[smem, vmem, hbm, hbm, hbm, vmem, vmem, vmem, vmem],
+            in_specs=[smem, vmem, hbm, hbm, hbm] + [hbm if mine else vmem] * 2 + [vmem, vmem],
             out_specs=[vmem if mine else hbm] * 2,
             out_shape=[shaped(*shape) if mine else pltpu.HBM(shape, BF16)] * 2,
             scratch_shapes=masks(rows)
@@ -501,19 +505,20 @@
             + [pltpu.VMEM((half_pairs, rows, 2 * HEAD), BF16)]
             + [pltpu.VMEM((half_pairs, 2, later, HEAD), BF16)] * 2
             + [dma(3, half_pairs)]
-            + ([] if mine else [pltpu.VMEM(shape, BF16)] * 2 + [dma(2, half_pairs)]),
+            + (
+                [pltpu.VMEM((half, CHUNK, HEAD), BF16)] * 2 + [dma(2)]
+                if mine
+                else [pltpu.VMEM(shape, BF16)] * 2 + [dma(2, half_pairs)]
+            ),
             compiler_params=params(24),
             name="attend",
         )(here, lengths, query_rows, pk_late, val_late, pk_first, val_first, rims, conv_weight)
 
     phi_other, mix_other = (in_hbm(x) for x in attend(False, pk_other, val_other))
-    phi_own, mix_own = attend(True, pk_own, val_own)
-
-    row_total = small(total_kernel, shaped(*spread.shape[1:], dtype=F32), gates, spread)
-    far = lax.ppermute(row_total, "x", [(1, 3)])
-    near = lax.ppermute(row_total, "x", [(i, i + 1) for i in range(x_count - 1)])
-    entering = small(enter_kernel, pltpu.HBM(spread.shape, BF16), gates, spread, near, far)
-    entered = lax.all_to_all(entering, "z", 0, 0, tiled=True).reshape(state)
+    phi_own, mix_own = attend(True, in_hbm(pk_own), in_hbm(val_own))
+
+    entering = small(enter_kernel, shaped(*spread.shape), gates, spread)
+    entered = lax.all_to_all(entering, ("x", "z"), 0, 0, tiled=True).reshape(state)
     carried_own, carried_other = small(
         lambda *r: carry_kernel(*r, chips=chips), [shaped(*state)] * 2, gates, entered, own, got
     )

time: 67 us -> 60.5 us (0.903)
  the two profiles are of different devices: /device:TPU:27 before, /device:TPU:1 now
where the time goes in v3:
time: 60.5 us; the launch traced here: 60.2 us
  blocking collectives  30.9 us (51%)
  Pallas kernels  21.7 us (36%)
  starting transfers between devices  7.47 us (12%)
    all_to_all x1, blocking collectives, per_device(): lax.all_to_all(chip_tail.reshape(chips, -1, HEAD), ('x', 'z'), 0, 0, tile...  17.6 us
    all_to_all x1, blocking collectives, per_device(): lax.all_to_all(entering, ('x', 'z'), 0, 0, tiled=True).reshape(state)  13.3 us
    pallas_call x2, Pallas kernels, attend(): pl.pallas_call(lambda *refs: attend_kernel(*refs, mine=mine), in_specs=[s...  8.44 us
    pallas_call x1, Pallas kernels, per_device(): pl.pallas_call(lambda *refs: late_kernel(*refs, chips=chips), in_specs=[s...  6.16 us
    pallas_call x2, Pallas kernels, finish(): pl.pallas_call(lambda *refs: finish_kernel(*refs, mine=mine, chips=chips)...  3.68 us
    ppermute x1, starting transfers between devices, per_device(): lax.ppermute(rims, CTX, [(i, (i + 1) % ctx_count) for i in range(ctx_coun...  3.02 us
    ppermute x1, starting transfers between devices, per_device(): carried_far = lax.ppermute(carried_other, 'c', swap)  2.8 us
    pallas_call x2, Pallas kernels, first(): pl.pallas_call(lambda *refs: first_kernel(*refs, mine=mine, rows=rows, ch...  2.43 us
  transfers between devices with their start and end apart: 3, of which 0 were waited for; matrix products, arithmetic and copies ran while one was open for 0% of the time, Pallas kernels for 29%

profile of v3, /device:TPU:1, one launch (start us, length us, event | category | flops | bytes accessed | tf_op | source)
XLA Modules:
  0.0 60.2 jit_solution(15460144119780954689)
XLA Ops:
  0.0 0.0 copy-start
  0.0 0.0 copy-start.4
  0.0 0.8 %rim.1 = bf16[3,8,1024]{2,1,0:T(8,128)(2,1)S(1)} custom-call(bf16[1024,1024]{1,0:T(8,128)(2,1)} %refs_2_.5, bf16[1024,1024]{1,0:T(8,128)(2,1)} %k_ref.1, bf16[1024,1024]{1,0:T(8,128)(2,1)} %v_ref.1), custom_call_target="tpu_custom_call" | custom-call | tf_op jit(solution)/shard_map/rim/pallas_call | solution.py:423
  0.8 3.0 %collective-permute-start = (bf16[3,8,1024]{2,1,0:T(8,128)(2,1)S(1)}, bf16[3,8,1024]{2,1,0:T(8,128)(2,1)S(1)}, u32[]{:S(2)}, u32[]{:S(2)}) collective-permute-start(bf16[3,8,1024]{2,1,0:T(8,128)(2,1)S(1)} %rim.1), channel_id=1, source_target_pairs={{0,1},{1,2},{2,3},{3,4},{4,5},{5,6},{6,7},{7,8},{8,9},{9,10},{10,1... | collective-permute-start | bytes 147464 | tf_op jit(solution)/shard_map/ppermute | solution.py:432
  3.8 0.0 copy-done
  3.8 0.0 copy-done.4
  3.8 6.2 %late.1 = (bf16[8,768,128]{2,1,0:T(8,128)(2,1)}, bf16[8,768,128]{2,1,0:T(8,128)(2,1)}, f32[8,3,128,128]{3,2,1,0:T(8,128)S(1)}, f32[48,128]{1,0:T(8,128)S(1)}, bf...) custom-call(s32[1]{0:T(128)} %bitcast.refs_0_, s32[1,128]{1,0:T(1,128)S(1)} %bitcast.9, ...), custom_call_target="tpu_custom_call" | custom-call | tf_op jit(solution)/shard_map/late/pallas_call | solution.py:450
  10.0 0.0 collective-permute-done.refs_5_.refs_7_
  10.0 1.2 %first.3 = (bf16[4,256,128]{2,1,0:T(8,128)(2,1)S(1)}, bf16[4,256,128]{2,1,0:T(8,128)(2,1)S(1)}, bf16[4,3,128,128]{3,2,1,0:T(8,128)(2,1)S(1)}, bf16[4,128,128]{2,1,0:T(8,128)(2,1)S(1)}) custom-call(s32[1]{0:T(128)} %bitcast.refs_0_, s32[1,128]{1,0:T(1,128)S(1)} %bitcast.10, f32[48,128]{1,0:T(8,128)S(1)} %get-tuple-element.28.refs_2_.r_0_.gate_ref.refs_1_, ...), custom_call_target="tpu_custom_call" | custom-call | tf_op jit(solution)/shard_map/first/pallas_call | solution.py:473
  11.2 1.7 %collective-permute-start.1 = (bf16[4,128,128]{2,1,0:T(8,128)(2,1)S(1)}, bf16[4,128,128]{2,1,0:T(8,128)(2,1)S(1)}, u32[]{:S(2)}, u32[]{:S(2)}) collective-permute-start(bf16[4,128,128]{2,1,0:T(8,128)(2,1)S(1)} %get-tuple-element.40), channel_id=1, source_target_pairs={{0,1},{1,0},{2,3},{3,2},{4,5},{5,4},{6,7},{7,6},{8,9},{9,8},{10,11... | collective-permute-start | bytes 393224 | tf_op jit(solution)/shard_map/ppermute | solution.py:489
  12.8 1.2 %first.2 = (bf16[4,256,128]{2,1,0:T(8,128)(2,1)S(1)}, bf16[4,256,128]{2,1,0:T(8,128)(2,1)S(1)}, bf16[4,3,128,128]{3,2,1,0:T(8,128)(2,1)S(1)}, bf16[4,128,128]{2,1,0:T(8,128)(2,1)S(1)}) custom-call(s32[1]{0:T(128)} %bitcast.refs_0_, s32[1,128]{1,0:T(1,128)S(1)} %bitcast.11, f32[48,128]{1,0:T(8,128)S(1)} %get-tuple-element.28.refs_2_.r_0_.gate_ref.refs_1_, ...), custom_call_target="tpu_custom_call" | custom-call | tf_op jit(solution)/shard_map/first/pallas_call | solution.py:473
  14.1 0.0 copy-start.1
  14.1 0.0 copy-start.2
  14.1 0.0 collective-permute-done.1.r_2_.r_3_
  14.1 0.1 shard_map.64
  14.2 17.6 %all_to_all.10.spread_ref = bf16[32,16,128]{2,1,0:T(8,128)(2,1)S(1)} all-to-all(bf16[32,16,128]{2,1,0:T(8,128)(2,1)S(1)} %bitcast.6), channel_id=1, replica_groups=mesh['dp'=4,'x'=4,'z'=8,'c'=2] {'x','z'}, dimensions={0} | all-to-all | bytes 262144 | tf_op jit(solution)/shard_map/all_to_all | solution.py:494
  31.8 0.1 shard_map.65
  31.8 13.3 %all_to_all.11 = bf16[32,16,128]{2,1,0:T(8,128)(2,1)S(1)} all-to-all(bf16[32,16,128]{2,1,0:T(8,128)(2,1)S(1)} %shard_map.65), channel_id=1, replica_groups=mesh['dp'=4,'x'=4,'z'=8,'c'=2] {'x','z'}, dimensions={0} | all-to-all | bytes 262144 | tf_op jit(solution)/shard_map/all_to_all | solution.py:521
  45.2 0.1 shard_map.66
  45.3 2.8 %collective-permute-start.2 = (bf16[4,128,128]{2,1,0:T(8,128)(2,1)S(1)}, bf16[4,128,128]{2,1,0:T(8,128)(2,1)S(1)}, u32[]{:S(2)}, u32[]{:S(2)}) collective-permute-start(bf16[4,128,128]{2,1,0:T(8,128)(2,1)S(1)} %get-tuple-element.49), channel_id=1, source_target_pairs={{0,1},{1,0},{2,3},{3,2},{4,5},{5,4},{6,7},{7,6},{8,9},{9,8},{10,11... | collective-permute-start | bytes 393224 | tf_op jit(solution)/shard_map/ppermute | solution.py:525
  48.1 0.0 copy-done.1
  48.1 0.0 copy-done.2
  48.1 4.0 %attend.2 = (bf16[4,1024,128]{2,1,0:T(8,128)(2,1)S(1)}, bf16[4,1024,128]{2,1,0:T(8,128)(2,1)S(1)}) custom-call(s32[1]{0:T(128)} %bitcast.refs_0_, s32[1,128]{1,0:T(1,128)S(1)} %bitcast.12, bf16[1024,1024]{1,0:T(8,128)(2,1)} %refs_2_.5, bf16[8,768,128]{2,1,0:T(8,128)(2,1)} %get-tuple-element.29.refs_3_, bf16[8,768,128]{2,1,0:T(8,128)(2,1)} %get-tuple-element.30.refs_4_, ...), custom_call_target="tpu_custom_call" | custom-call | tf_op jit(solution)/shard_map/attend/pallas_call | solution.py:498
  52.1 0.0 copy-start.3
  52.1 4.4 %attend.3 = (bf16[4,1024,128]{2,1,0:T(8,128)(2,1)}, bf16[4,1024,128]{2,1,0:T(8,128)(2,1)}) custom-call(s32[1]{0:T(128)} %bitcast.refs_0_, s32[1,128]{1,0:T(1,128)S(1)} %bitcast.13, bf16[1024,1024]{1,0:T(8,128)(2,1)} %refs_2_.5, bf16[8,768,128]{2,1,0:T(8,128)(2,1)} %get-tuple-element.29.refs_3_, bf16[8,768,128]{2,1,0:T(8,128)(2,1)} %get-tuple-element.30.refs_4_, ...), custom_call_target="tpu_custom_call" | custom-call | tf_op jit(solution)/shard_map/attend/pallas_call | solution.py:498
  56.5 0.0 copy-done.3
  56.5 1.8 %finish.2 = (bf16[1024,1024]{1,0:T(8,128)(2,1)}, bf16[4,1024,128]{2,1,0:T(8,128)(2,1)S(1)}, bf16[4,1024,128]{2,1,0:T(8,128)(2,1)S(1)}) custom-call(s32[1]{0:T(128)} %bitcast.refs_0_, f32[48,128]{1,0:T(8,128)S(1)} %get-tuple-element.28.refs_2_.r_0_.gate_ref.refs_1_, bf16[4,1024,128]{2,1,0:T(8,128)(2,1)S(1)} %get-tuple-element.36.refs_2_, ...), custom_call_target="tpu_custom_call" | custom-call | tf_op jit(solution)/shard_map/finish/pallas_call | solution.py:531
  58.4 0.0 collective-permute-done.2.refs_5_
  58.4 1.8 %finish.3 = bf16[1024,1024]{1,0:T(8,128)(2,1)} custom-call(s32[1]{0:T(128)} %bitcast.refs_0_, f32[48,128]{1,0:T(8,128)S(1)} %get-tuple-element.28.refs_2_.r_0_.gate_ref.refs_1_, bf16[4,1024,128]{2,1,0:T(8,128)(2,1)S(1)} %get-tuple-element.46.refs_2_, bf16[4,1024,128]{2,1,0:T(8,128)(2,1)S(1)} %get-tuple-element.47.refs_3_, ...), custom_call_target="tpu_custom_call", output_to_operand_aliasing={{}: (7, {})} | custom-call | tf_op jit(solution)/shard_map/finish/pallas_call | solution.py:531
Async XLA Ops:
  0.0 3.8 %copy-start = (f32[3,4,1024]{2,1,0:T(4,128)S(1)}, f32[3,4,1024]{2,1,0:T(4,128)}, u32[]{:S(2)}) copy-start(f32[3,4,1024]{2,1,0:T(4,128)} %refs_8_.3) | copy-start | bytes 147460
  0.0 3.8 %copy-start.4 = (s32[128]{0:T(128)S(1)}, s32[128]{0:T(128)}, u32[]{:S(2)}) copy-start(s32[128]{0:T(128)} %param.9) | copy-start | bytes 1540
  0.8 9.2 %collective-permute-start = (bf16[3,8,1024]{2,1,0:T(8,128)(2,1)S(1)}, bf16[3,8,1024]{2,1,0:T(8,128)(2,1)S(1)}, u32[]{:S(2)}, u32[]{:S(2)}) collective-permute-start(bf16[3,8,1024]{2,1,0:T(8,128)(2,1)S(1)} %rim.1), channel_id=1, source_target_pairs={{0,1},{1,2},{2,3},{3,4},{4,5},{5,6},{6,7},{7,8},{8,9},{9,10},{10,1... | collective-permute-start | bytes 147464 | tf_op jit(solution)/shard_map/ppermute | solution.py:432
  11.2 2.9 %collective-permute-start.1 = (bf16[4,128,128]{2,1,0:T(8,128)(2,1)S(1)}, bf16[4,128,128]{2,1,0:T(8,128)(2,1)S(1)}, u32[]{:S(2)}, u32[]{:S(2)}) collective-permute-start(bf16[4,128,128]{2,1,0:T(8,128)(2,1)S(1)} %get-tuple-element.40), channel_id=1, source_target_pairs={{0,1},{1,0},{2,3},{3,2},{4,5},{5,4},{6,7},{7,6},{8,9},{9,8},{10,11... | collective-permute-start | bytes 393224 | tf_op jit(solution)/shard_map/ppermute | solution.py:489
  14.1 34.0 %copy-start.1 = (bf16[4,256,128]{2,1,0:T(8,128)(2,1)}, bf16[4,256,128]{2,1,0:T(8,128)(2,1)S(1)}, u32[]{:S(2)}) copy-start(bf16[4,256,128]{2,1,0:T(8,128)(2,1)S(1)} %get-tuple-element.34.refs_5_) | copy-start | bytes 786436
  14.1 34.0 %copy-start.2 = (bf16[4,256,128]{2,1,0:T(8,128)(2,1)}, bf16[4,256,128]{2,1,0:T(8,128)(2,1)S(1)}, u32[]{:S(2)}) copy-start(bf16[4,256,128]{2,1,0:T(8,128)(2,1)S(1)} %get-tuple-element.35.refs_6_) | copy-start | bytes 786436
  45.3 13.1 %collective-permute-start.2 = (bf16[4,128,128]{2,1,0:T(8,128)(2,1)S(1)}, bf16[4,128,128]{2,1,0:T(8,128)(2,1)S(1)}, u32[]{:S(2)}, u32[]{:S(2)}) collective-permute-start(bf16[4,128,128]{2,1,0:T(8,128)(2,1)S(1)} %get-tuple-element.49), channel_id=1, source_target_pairs={{0,1},{1,0},{2,3},{3,2},{4,5},{5,4},{6,7},{7,6},{8,9},{9,8},{10,11... | collective-permute-start | bytes 393224 | tf_op jit(solution)/shard_map/ppermute | solution.py:525
  52.1 4.4 %copy-start.3 = (f32[1024]{0:T(1024)S(1)}, f32[1024]{0:T(1024)}, u32[]{:S(2)}) copy-start(f32[1024]{0:T(1024)} %param.11) | copy-start | bytes 12292

commit v4 on v3

--- a/solution.py
+++ b/solution.py
@@ -9,6 +9,7 @@
 HEAD = 128
 CHUNK = 256
 GROUP = 16
+BLOCK = 256
 CTX = ("x", "z", "c")
 DP_CTX = ("dp", "x", "z", "c")
 F32 = jnp.float32
@@ -89,7 +90,7 @@
 
 def late_kernel(
     here_ref, len_ref, k_hbm, v_hbm, w_ref,
-    pk_hbm, val_hbm, st_ref, gate_ref, k0_ref, v0_ref,
+    pk_hbm, val_hbm, st_ref, gate_ref, k0_ref, v0_ref, m0_ref, live0_ref,
     doc_s, m_s, live_s, ext_k, ext_v, kb, vb, pkb, valb, in_sem, out_sem, edge_sem,
     *, chips,
 ):
@@ -98,8 +99,11 @@
     pairs = kb.shape[0]
     tail_rows = pl.ds(CHUNK - GROUP, rows - CHUNK + GROUP)
 
+    def head_of(p):
+        return 2 * ((p + (1 - here_ref[0] % 2) * (pairs // 2)) % pairs)
+
     def fetch(p):
-        cols = lanes(2 * p, 2)
+        cols = lanes(head_of(p), 2)
         return [
             pltpu.make_async_copy(k_hbm.at[tail_rows, cols], kb.at[p], in_sem.at[0, p]),
             pltpu.make_async_copy(v_hbm.at[tail_rows, cols], vb.at[p], in_sem.at[1, p]),
@@ -126,6 +130,8 @@
     starts = starts_of(len_ref[...])
     fill_doc(offset, starts, doc_s, m_s)
     fill_live(doc_s, live_s)
+    m0_ref[...] = m_s[:, :CHUNK]
+    live0_ref[...] = live_s[:CHUNK]
     chip = offset - core * rows
     chip_mark = lax.broadcasted_iota(jnp.int32, (chips + 8, HEAD), 0)
     mark = lax.broadcasted_iota(jnp.int32, (16, HEAD), 0)
@@ -159,7 +165,8 @@
             cols = slice(n * HEAD, (n + 1) * HEAD)
             ext_k[n, CHUNK - 8 :] = kb[p, :, cols].astype(F32)
             ext_v[n, CHUNK - 8 :] = vb[p, :, cols].astype(F32)
-        taps = [(0.5 * w_ref[1, :, lanes(2 * p + n)], w_ref[2, :, lanes(2 * p + n)]) for n in (0, 1)]
+        head = head_of(p)
+        taps = [(0.5 * w_ref[1, :, lanes(head + n)], w_ref[2, :, lanes(head + n)]) for n in (0, 1)]
         states = [jnp.zeros((HEAD, HEAD), F32)] * 2
         for i in range(1, chunks):
             r0 = i * CHUNK
@@ -169,25 +176,26 @@
                 pkb[2 * p + n, r0 - CHUNK : r0] = key
                 valb[2 * p + n, r0 - CHUNK : r0] = val
                 states[n] = states[n] * same + tail
-                st_ref[2 * p + n, i - 1] = states[n]
-        run(store(p))
+                st_ref[head + n, i - 1] = states[n]
+
+        @pl.when(p < pairs // 2)
+        def _():
+            run(store(p))
 
     finish_all(edges)
-    for p in range(pairs):
+    for p in range(pairs // 2):
         finish_all(store(p))
 
 
 def first_kernel(
-    here_ref, len_ref, gate_ref, k_ref, v_ref, rim_ref, w_ref, late_ref,
-    pk_ref, val_ref, st_ref, tail_ref, doc_s, m_s, live_s, ext_k, ext_v,
-    *, mine, rows, chips,
+    here_ref, gate_ref, k_ref, v_ref, m_ref, live_ref, rim_ref, w_ref, late_ref,
+    st_ref, tail_ref, ext_k, ext_v,
+    *, mine, chips,
 ):
-    heads = pk_ref.shape[0]
+    heads = tail_ref.shape[0]
     here = here_ref[0]
     base = (here % 2 if mine else 1 - here % 2) * heads
     count = late_ref.shape[1] + 1
-    fill_doc(here * rows, starts_of(len_ref[...]), doc_s, m_s)
-    fill_live(doc_s, live_s)
 
     @pl.loop(0, heads // 2)
     def _(p):
@@ -200,11 +208,9 @@
         for n in (0, 1):
             h = 2 * p + n
             cols = lanes(base + h)
-            key, val, tail = kv_chunk(
-                ext_k.at[n], ext_v.at[n], 0.5 * w_ref[1, :, cols], w_ref[2, :, cols], m_s, live_s, 0
+            _, _, tail = kv_chunk(
+                ext_k.at[n], ext_v.at[n], 0.5 * w_ref[1, :, cols], w_ref[2, :, cols], m_ref, live_ref, 0
             )
-            pk_ref[h] = key
-            val_ref[h] = val
             st_ref[h, 0] = tail.astype(BF16)
             for i in range(1, count):
                 state = late_ref[base + h, i - 1] + tail * gate_ref[chips + 10 + i : chips + 11 + i]
@@ -214,42 +220,39 @@
 
 
 def attend_kernel(
-    here_ref, len_ref, q_hbm, pkl_hbm, vall_hbm, pkf_ref, valf_ref, rim_ref, w_ref,
-    pq_out, mix_out, doc_s, m_s, use_s, ext, allow_s, qb, kb, vb, in_sem, *staging,
-    mine,
+    here_ref, len_ref, q_hbm, k_hbm, v_hbm, rim_ref, w_ref, *rest, mine,
 ):
-    heads, rows, _ = pq_out.shape
+    if mine:
+        pq_ref, mix_ref, doc_s, m_s, use_s, ext, ext_k, ext_v, allow_s, qb, k0b, v0b, in_sem = rest
+    else:
+        (pk_hbm, val_hbm, pq_out, mix_out, doc_s, m_s, use_s, ext, ext_k, ext_v, allow_s,
+         qb, k0b, v0b, in_sem, kb, vb, pq_ref, mix_ref, late_sem, out_sem) = rest
+    pairs, rows, _ = pq_ref.shape
     chunks = rows // CHUNK
-    pairs = heads // 2
     here = here_ref[0]
-    base = (here % 2 if mine else 1 - here % 2) * heads
-    if mine:
-        kf_s, vf_s, first_sem = staging
-        firsts = [
-            pltpu.make_async_copy(pkf_ref, kf_s, first_sem.at[0]),
-            pltpu.make_async_copy(valf_ref, vf_s, first_sem.at[1]),
+    base = (here % 2 if mine else 1 - here % 2) * 2 * pairs
+    made = pl.ds(0, k0b.shape[1])
+
+    def fetch(p):
+        cols, two = lanes(base + 2 * p, 2), pl.ds(2 * p, 2)
+        copies = [
+            pltpu.make_async_copy(q_hbm.at[:, cols], qb.at[p], in_sem.at[0, p]),
+            pltpu.make_async_copy(k_hbm.at[made, cols], k0b.at[p], in_sem.at[1, p]),
+            pltpu.make_async_copy(v_hbm.at[made, cols], v0b.at[p], in_sem.at[2, p]),
         ]
-        pq_ref, mix_ref, pkf_ref, valf_ref = pq_out, mix_out, kf_s, vf_s
-    else:
-        firsts = []
-        pq_ref, mix_ref, out_sem = staging
-
-    def fetch(p):
-        two = pl.ds(base + 2 * p, 2)
+        if not mine:
+            copies += [
+                pltpu.make_async_copy(pk_hbm.at[two], kb.at[p], late_sem.at[0, p]),
+                pltpu.make_async_copy(val_hbm.at[two], vb.at[p], late_sem.at[1, p]),
+            ]
+        return copies
+
+    def store(p):
         return [
-            pltpu.make_async_copy(q_hbm.at[:, lanes(base + 2 * p, 2)], qb.at[p], in_sem.at[0, p]),
-            pltpu.make_async_copy(pkl_hbm.at[two], kb.at[p], in_sem.at[1, p]),
-            pltpu.make_async_copy(vall_hbm.at[two], vb.at[p], in_sem.at[2, p]),
+            pltpu.make_async_copy(pq_ref.at[p], pq_out.at[p], out_sem.at[0, p]),
+            pltpu.make_async_copy(mix_ref.at[p], mix_out.at[p], out_sem.at[1, p]),
         ]
 
-    def store(p):
-        two = pl.ds(2 * p, 2)
-        return [
-            pltpu.make_async_copy(pq_ref.at[two], pq_out.at[two], out_sem.at[0, p]),
-            pltpu.make_async_copy(mix_ref.at[two], mix_out.at[two], out_sem.at[1, p]),
-        ]
-
-    run(firsts)
     for p in range(pairs):
         run(fetch(p))
 
@@ -266,38 +269,43 @@
         same = wide(doc) == across[0:1, r0 : r0 + CHUNK]
         allow_s[i] = jnp.where(same & causal, 1.0, 0.0).astype(BF16)
         use_s[r0 : r0 + CHUNK] = one_if(doc == doc_s[8 + r0 - 1 : 8 + r0]).astype(BF16)
-    finish_all(firsts)
 
     @pl.loop(0, pairs)
     def _(p):
         finish_all(fetch(p))
+        taps = []
         for n in (0, 1):
-            ext[n, 0:8] = rim_ref[0, :, lanes(base + 2 * p + n)].astype(F32)
-            ext[n, 8:] = qb[p, :, n * HEAD : (n + 1) * HEAD].astype(F32)
-        taps = [0.5 * w_ref[0, :, lanes(base + 2 * p + n)] for n in (0, 1)]
+            cols, head = slice(n * HEAD, (n + 1) * HEAD), lanes(base + 2 * p + n)
+            for which, buffer, rows in ((0, ext, qb), (1, ext_k, k0b), (2, ext_v, v0b)):
+                buffer[n, 0:8] = rim_ref[which, :, head].astype(F32)
+                buffer[n, 8:] = rows[p, :, cols].astype(F32)
+            taps.append((0.5 * w_ref[0, :, head], 0.5 * w_ref[1, :, head], w_ref[2, :, head]))
 
         def make(i, n):
-            rows = slice(i * CHUNK, (i + 1) * CHUNK)
-            query = silu_of_half(conv(ext.at[n], taps[n], m_s, i * CHUNK)).astype(BF16)
-            pq_ref[2 * p + n, rows] = query * use_s[rows]
-            return query
-
-        def mixed(i, n, query):
             r0 = i * CHUNK
-            key = pkf_ref[2 * p + n] if i == 0 else kb[p, n, r0 - CHUNK : r0]
-            val = valf_ref[2 * p + n] if i == 0 else vb[p, n, r0 - CHUNK : r0]
+            rows = slice(r0, r0 + CHUNK)
+            query = silu_of_half(conv(ext.at[n], taps[n][0], m_s, r0)).astype(BF16)
+            pq_ref[p, rows, n * HEAD : (n + 1) * HEAD] = query * use_s[rows]
+            if mine or i == 0:
+                key = silu_of_half(conv(ext_k.at[n], taps[n][1], m_s, r0)).astype(BF16)
+                val = conv(ext_v.at[n], taps[n][2], m_s, r0).astype(BF16)
+            else:
+                key, val = kb[p, n, r0 - CHUNK : r0], vb[p, n, r0 - CHUNK : r0]
+            return query, key, val
+
+        def mixed(i, n, query, key, val):
             scores = lax.dot_general(query, key, (((1,), (1,)), ((), ())), preferred_element_type=F32)
             weights = scores.astype(BF16) * allow_s[i]
             mix = jnp.dot(weights, val, preferred_element_type=F32)
-            mix_ref[2 * p + n, r0 : r0 + CHUNK] = mix.astype(BF16)
+            mix_ref[p, i * CHUNK : (i + 1) * CHUNK, n * HEAD : (n + 1) * HEAD] = mix.astype(BF16)
 
         ahead = None
         for i in range(chunks):
             for n in (0, 1):
-                query = make(i, n)
+                made_now = make(i, n)
                 if ahead is not None:
                     mixed(*ahead)
-                ahead = (i, n, query)
+                ahead = (i, n) + made_now
         mixed(*ahead)
         if not mine:
             run(store(p))
@@ -305,6 +313,13 @@
     if not mine:
         for p in range(pairs):
             finish_all(store(p))
+
+
+def both(first, second):
+    none = jnp.zeros_like(first)
+    return jnp.concatenate(
+        [jnp.concatenate([first, none], axis=1), jnp.concatenate([none, second], axis=1)], axis=0
+    )
 
 
 def finish_kernel(here_ref, gate_ref, pq_ref, mix_ref, st_ref, carried_ref, gain_ref, *rest, mine, chips):
@@ -317,10 +332,10 @@
     else:
         _, out_hbm, outb, out_sem = rest
         onward = []
-    heads, rows, _ = pq_ref.shape
+    pairs, rows, _ = pq_ref.shape
     chunks = rows // CHUNK
-    base = (here_ref[0] % 2 if mine else 1 - here_ref[0] % 2) * heads
-    mean = jnp.full((HEAD, HEAD), 1.0 / HEAD, BF16)
+    base = (here_ref[0] % 2 if mine else 1 - here_ref[0] % 2) * 2 * pairs
+    mean = both(jnp.full((HEAD, HEAD), 1.0 / HEAD, BF16), jnp.full((HEAD, HEAD), 1.0 / HEAD, BF16))
     run(onward)
 
     def store(p, i):
@@ -329,37 +344,39 @@
             outb.at[p, rows], out_hbm.at[rows, lanes(base + 2 * p, 2)], out_sem.at[p, i]
         )
 
-    @pl.loop(0, heads // 2)
+    @pl.loop(0, pairs)
     def _(p):
-        gain = [gain_ref[:, lanes(base + 2 * p + n)] for n in (0, 1)]
-
-        def blend(i, n):
-            h = 2 * p + n
-            state = carried_ref[h].astype(F32)
-            if i:
-                state = st_ref[h, i - 1].astype(F32) + state * gate_ref[chips + 7 + i : chips + 8 + i]
-            rows = slice(i * CHUNK, (i + 1) * CHUNK)
-            held = jnp.dot(pq_ref[h, rows], state.astype(BF16), preferred_element_type=F32)
-            return mix_ref[h, rows].astype(F32) + held
-
-        def norm(i, n, mixture):
+        gain = gain_ref[:, lanes(base + 2 * p, 2)]
+
+        def entering(h, i):
+            if not i:
+                return carried_ref[h]
+            kept = carried_ref[h].astype(F32) * gate_ref[chips + 7 + i : chips + 8 + i]
+            return (st_ref[h, i - 1].astype(F32) + kept).astype(BF16)
+
+        def blend(at, state):
+            held = jnp.dot(pq_ref[p, at : at + BLOCK], state, preferred_element_type=F32)
+            return mix_ref[p, at : at + BLOCK].astype(F32) + held
+
+        def norm(at, mixture):
             square = jnp.dot((mixture * mixture).astype(BF16), mean, preferred_element_type=F32)
-            scale = lax.rsqrt(square + 1e-06) * gain[n]
-            outb[p, i * CHUNK : (i + 1) * CHUNK, n * HEAD : (n + 1) * HEAD] = (mixture * scale).astype(BF16)
-            if n:
-                store(p, i).start()
+            scale = lax.rsqrt(square + 1e-06) * gain
+            outb[p, at : at + BLOCK] = (mixture * scale).astype(BF16)
+            if (at + BLOCK) % CHUNK == 0:
+                store(p, at // CHUNK).start()
 
         ahead = None
         for i in range(chunks):
-            for n in (0, 1):
-                mixture = blend(i, n)
+            state = both(entering(2 * p, i), entering(2 * p + 1, i))
+            for at in range(i * CHUNK, (i + 1) * CHUNK, BLOCK):
+                mixture = blend(at, state)
                 if ahead is not None:
                     norm(*ahead)
-                ahead = (i, n, mixture)
+                ahead = (at, mixture)
         norm(*ahead)
 
     finish_all(onward)
-    for p in range(heads // 2):
+    for p in range(pairs):
         for i in range(chunks):
             store(p, i).wait()
 
@@ -447,23 +464,25 @@
             pltpu.VMEM((count, HEAD), BF16),
         ]
 
-    pk_late, val_late, st_late, gates, key_head, value_head = pl.pallas_call(
+    pk_late, val_late, st_late, gates, key_head, value_head, inside, live = pl.pallas_call(
         lambda *refs: late_kernel(*refs, chips=chips),
         in_specs=[smem, vmem, hbm, hbm, vmem],
-        out_specs=[hbm, hbm, vmem, vmem, vmem, vmem],
+        out_specs=[hbm, hbm] + [vmem] * 6,
         out_shape=[
-            pltpu.HBM((heads, later, HEAD), BF16),
-            pltpu.HBM((heads, later, HEAD), BF16),
+            pltpu.HBM((half, later, HEAD), BF16),
+            pltpu.HBM((half, later, HEAD), BF16),
             shaped(heads, chunks - 1, HEAD, HEAD, dtype=F32),
             shaped(gate_rows, HEAD, dtype=F32),
             shaped(CHUNK, channels),
             shaped(CHUNK, channels),
+            shaped(3, CHUNK, HEAD, dtype=F32),
+            shaped(CHUNK, HEAD),
         ],
         scratch_shapes=masks(rows)
         + [pltpu.VMEM((2, rows + 8, HEAD), F32)] * 2
         + [pltpu.VMEM((pairs, later + GROUP, 2 * HEAD), BF16)] * 2
         + [pltpu.VMEM((heads, later, HEAD), BF16)] * 2
-        + [dma(2, pairs), dma(2, pairs), dma(2)],
+        + [dma(2, pairs), dma(2, half_pairs), dma(2)],
         compiler_params=params(20),
         name="late",
     )(here, lengths, key_rows, value_rows, conv_weight)
@@ -471,51 +490,53 @@
 
     def first(mine):
         return pl.pallas_call(
-            lambda *refs: first_kernel(*refs, mine=mine, rows=rows, chips=chips),
-            in_specs=[smem] + [vmem] * 7,
-            out_specs=[vmem] * 4,
+            lambda *refs: first_kernel(*refs, mine=mine, chips=chips),
+            in_specs=[smem] + [vmem] * 8,
+            out_specs=[vmem] * 2,
             out_shape=[
-                shaped(half, CHUNK, HEAD),
-                shaped(half, CHUNK, HEAD),
                 shaped(half, chunks - 1, HEAD, HEAD),
                 shaped(half, HEAD, HEAD),
             ],
-            scratch_shapes=masks(CHUNK) + [pltpu.VMEM((2, CHUNK + 8, HEAD), F32)] * 2,
+            scratch_shapes=[pltpu.VMEM((2, CHUNK + 8, HEAD), F32)] * 2,
             compiler_params=params(8),
             name="first",
-        )(here, lengths, gates, key_head, value_head, rims, conv_weight, st_late)
-
-    pk_other, val_other, inner_other, other = first(False)
+        )(here, gates, key_head, value_head, inside, live, rims, conv_weight, st_late)
+
+    inner_other, other = first(False)
     got = lax.ppermute(other, "c", swap)
-    pk_own, val_own, inner_own, own = first(True)
+    inner_own, own = first(True)
 
     state = (half, HEAD, HEAD)
     chip_tail = small(lambda *r: join_kernel(*r, chips=chips), shaped(*state), gates, own, got)
     spread = lax.all_to_all(chip_tail.reshape(chips, -1, HEAD), ("x", "z"), 0, 0, tiled=True)
 
-    def attend(mine, pk_first, val_first):
-        shape = (half, rows, HEAD)
+    def attend(mine, *ready):
+        shape = (half_pairs, rows, 2 * HEAD)
+        made = rows if mine else CHUNK
         return pl.pallas_call(
             lambda *refs: attend_kernel(*refs, mine=mine),
-            in_specs=[smem, vmem, hbm, hbm, hbm] + [hbm if mine else vmem] * 2 + [vmem, vmem],
+            in_specs=[smem, vmem, hbm, hbm, hbm, vmem, vmem] + [hbm] * len(ready),
             out_specs=[vmem if mine else hbm] * 2,
             out_shape=[shaped(*shape) if mine else pltpu.HBM(shape, BF16)] * 2,
             scratch_shapes=masks(rows)
-            + [pltpu.VMEM((2, rows + 8, HEAD), F32), pltpu.VMEM((chunks, CHUNK, CHUNK), BF16)]
-            + [pltpu.VMEM((half_pairs, rows, 2 * HEAD), BF16)]
-            + [pltpu.VMEM((half_pairs, 2, later, HEAD), BF16)] * 2
+            + [pltpu.VMEM((2, rows + 8, HEAD), F32)]
+            + [pltpu.VMEM((2, made + 8, HEAD), F32)] * 2
+            + [pltpu.VMEM((chunks, CHUNK, CHUNK), BF16), pltpu.VMEM(shape, BF16)]
+            + [pltpu.VMEM((half_pairs, made, 2 * HEAD), BF16)] * 2
             + [dma(3, half_pairs)]
             + (
-                [pltpu.VMEM((half, CHUNK, HEAD), BF16)] * 2 + [dma(2)]
+                []
                 if mine
-                else [pltpu.VMEM(shape, BF16)] * 2 + [dma(2, half_pairs)]
+                else [pltpu.VMEM((half_pairs, 2, later, HEAD), BF16)] * 2
+                + [pltpu.VMEM(shape, BF16)] * 2
+                + [dma(2, half_pairs)] * 2
             ),
             compiler_params=params(24),
             name="attend",
-        )(here, lengths, query_rows, pk_late, val_late, pk_first, val_first, rims, conv_weight)
-
-    phi_other, mix_other = (in_hbm(x) for x in attend(False, pk_other, val_other))
-    phi_own, mix_own = attend(True, in_hbm(pk_own), in_hbm(val_own))
+        )(here, lengths, query_rows, key_rows, value_rows, rims, conv_weight, *ready)
+
+    phi_other, mix_other = (in_hbm(x) for x in attend(False, pk_late, val_late))
+    phi_own, mix_own = attend(True)
 
     entering = small(enter_kernel, shaped(*spread.shape), gates, spread)
     entered = lax.all_to_all(entering, ("x", "z"), 0, 0, tiled=True).reshape(state)
@@ -525,7 +546,7 @@
     carried_far = lax.ppermute(carried_other, "c", swap)
 
     def finish(mine, phi, mix, inner, carried, *others):
-        shape = (half, rows, HEAD)
+        shape = (half_pairs, rows, 2 * HEAD)
         ahead = [shaped(*shape)] * 2 if mine else []
         args = (here, gates, phi, mix, inner, carried, gains, *others)
         return pl.pallas_call(

time: 60.5 us -> 62 us (1.025)
  Pallas kernels: 21.7 us -> 22.9 us
    pallas_call x2, Pallas kernels: 8.44 us -> 10.7 us  [attend(): pl.pallas_call(lambda *refs: attend_kernel(*refs, mine=mine), in_specs=[s...]
    pallas_call x2, Pallas kernels: 2.43 us -> 1.79 us  [first(): pl.pallas_call(lambda *refs: first_kernel(*refs, mine=mine, chips=chips),...]
  transfers between devices with their start and end apart: 3 -> 3, of which waited for: 0 -> 1; matrix products, arithmetic and copies ran while one was open for 0% -> 0% of each run, Pallas kernels for 29% -> 31%
where the time goes in v4:
time: 62 us; the launch traced here: 61.8 us
  blocking collectives  30.8 us (50%)
  Pallas kernels  22.9 us (37%)
  starting transfers between devices  7.93 us (13%)
    all_to_all x1, blocking collectives, per_device(): lax.all_to_all(chip_tail.reshape(chips, -1, HEAD), ('x', 'z'), 0, 0, tile...  17.4 us
    all_to_all x1, blocking collectives, per_device(): lax.all_to_all(entering, ('x', 'z'), 0, 0, tiled=True).reshape(state)  13.4 us
    pallas_call x2, Pallas kernels, attend(): pl.pallas_call(lambda *refs: attend_kernel(*refs, mine=mine), in_specs=[s...  10.7 us
    pallas_call x1, Pallas kernels, per_device(): pl.pallas_call(lambda *refs: late_kernel(*refs, chips=chips), in_specs=[s...  5.66 us
    pallas_call x2, Pallas kernels, finish(): pl.pallas_call(lambda *refs: finish_kernel(*refs, mine=mine, chips=chips)...  3.73 us
    ppermute x1, starting transfers between devices, per_device(): lax.ppermute(rims, CTX, [(i, (i + 1) % ctx_count) for i in range(ctx_coun...  3.02 us
    ppermute x1, starting transfers between devices, per_device(): carried_far = lax.ppermute(carried_other, 'c', swap)  2.77 us
    ppermute x1, starting transfers between devices, per_device(): got = lax.ppermute(other, 'c', swap)  2.14 us
  transfers between devices with their start and end apart: 3, of which 1 were waited for; matrix products, arithmetic and copies ran while one was open for 0% of the time, Pallas kernels for 31%

profile of v4, /device:TPU:1, one launch (start us, length us, event | category | flops | bytes accessed | tf_op | source)
XLA Modules:
  0.0 61.8 jit_solution(2727672450046240542)
XLA Ops:
  0.0 0.0 copy-start
  0.0 0.0 copy-start.2
  0.0 0.8 %rim.1 = bf16[3,8,1024]{2,1,0:T(8,128)(2,1)S(1)} custom-call(bf16[1024,1024]{1,0:T(8,128)(2,1)} %refs_2_.5, bf16[1024,1024]{1,0:T(8,128)(2,1)} %refs_3_.5, bf16[1024,1024]{1,0:T(8,128)(2,1)} %refs_4_.5), custom_call_target="tpu_custom_call" | custom-call | tf_op jit(solution)/shard_map/rim/pallas_call | solution.py:440
  0.8 3.0 %collective-permute-start = (bf16[3,8,1024]{2,1,0:T(8,128)(2,1)S(1)}, bf16[3,8,1024]{2,1,0:T(8,128)(2,1)S(1)}, u32[]{:S(2)}, u32[]{:S(2)}) collective-permute-start(bf16[3,8,1024]{2,1,0:T(8,128)(2,1)S(1)} %rim.1), channel_id=1, source_target_pairs={{0,1},{1,2},{2,3},{3,4},{4,5},{5,6},{6,7},{7,8},{8,9},{9,10},{10,1... | collective-permute-start | bytes 147464 | tf_op jit(solution)/shard_map/ppermute | solution.py:449
  3.8 0.0 copy-done
  3.8 0.0 copy-done.2
  3.8 5.7 %late.1 = (bf16[4,768,128]{2,1,0:T(8,128)(2,1)}, bf16[4,768,128]{2,1,0:T(8,128)(2,1)}, f32[8,3,128,128]{3,2,1,0:T(8,128)S(1)}, f32[48,128]{1,0:T(8,128)S(1)}, bf...) custom-call(s32[1]{0:T(128)} %bitcast.refs_0_, ...), custom_call_target="tpu_custom_call" | custom-call | tf_op jit(solution)/shard_map/late/pallas_call | solution.py:467
  9.5 0.0 collective-permute-done.refs_5_.refs_6_
  9.5 0.9 %first.3 = (bf16[4,3,128,128]{3,2,1,0:T(8,128)(2,1)S(1)}, bf16[4,128,128]{2,1,0:T(8,128)(2,1)S(1)}) custom-call(s32[1]{0:T(128)} %bitcast.refs_0_, f32[48,128]{1,0:T(8,128)S(1)} %get-tuple-element.26.refs_1_.r_0_.gate_ref, bf16[256,1024]{1,0:T(8,128)(2,1)S(1)} %get-tuple-element.29.refs_2_, bf16[256,1024]{1,0:T(8,128)(2,1)S(1)} %get-tuple-element.30.refs_3_, ...), custom_call_target="tpu_custom_call" | custom-call | tf_op jit(solution)/shard_map/first/pallas_call | solution.py:492
  10.4 2.1 %collective-permute-start.1 = (bf16[4,128,128]{2,1,0:T(8,128)(2,1)S(1)}, bf16[4,128,128]{2,1,0:T(8,128)(2,1)S(1)}, u32[]{:S(2)}, u32[]{:S(2)}) collective-permute-start(bf16[4,128,128]{2,1,0:T(8,128)(2,1)S(1)} %get-tuple-element.36), channel_id=1, source_target_pairs={{0,1},{1,0},{2,3},{3,2},{4,5},{5,4},{6,7},{7,6},{8,9},{9,8},{10,11... | collective-permute-start | bytes 393224 | tf_op jit(solution)/shard_map/ppermute | solution.py:506
  12.5 0.9 %first.2 = (bf16[4,3,128,128]{3,2,1,0:T(8,128)(2,1)S(1)}, bf16[4,128,128]{2,1,0:T(8,128)(2,1)S(1)}) custom-call(s32[1]{0:T(128)} %bitcast.refs_0_, f32[48,128]{1,0:T(8,128)S(1)} %get-tuple-element.26.refs_1_.r_0_.gate_ref, bf16[256,1024]{1,0:T(8,128)(2,1)S(1)} %get-tuple-element.29.refs_2_, bf16[256,1024]{1,0:T(8,128)(2,1)S(1)} %get-tuple-element.30.refs_3_, ...), custom_call_target="tpu_custom_call" | custom-call | tf_op jit(solution)/shard_map/first/pallas_call | solution.py:492
  13.4 0.1 collective-permute-done.1.r_2_.r_3_
  13.5 0.1 shard_map.64
  13.6 17.4 %all_to_all.10.spread_ref = bf16[32,16,128]{2,1,0:T(8,128)(2,1)S(1)} all-to-all(bf16[32,16,128]{2,1,0:T(8,128)(2,1)S(1)} %bitcast.6), channel_id=1, replica_groups=mesh['dp'=4,'x'=4,'z'=8,'c'=2] {'x','z'}, dimensions={0} | all-to-all | bytes 262144 | tf_op jit(solution)/shard_map/all_to_all | solution.py:511
  31.0 0.1 shard_map.65
  31.0 13.4 %all_to_all.11 = bf16[32,16,128]{2,1,0:T(8,128)(2,1)S(1)} all-to-all(bf16[32,16,128]{2,1,0:T(8,128)(2,1)S(1)} %shard_map.65), channel_id=1, replica_groups=mesh['dp'=4,'x'=4,'z'=8,'c'=2] {'x','z'}, dimensions={0} | all-to-all | bytes 262144 | tf_op jit(solution)/shard_map/all_to_all | solution.py:542
  44.4 0.1 shard_map.66
  44.5 2.8 %collective-permute-start.2 = (bf16[4,128,128]{2,1,0:T(8,128)(2,1)S(1)}, bf16[4,128,128]{2,1,0:T(8,128)(2,1)S(1)}, u32[]{:S(2)}, u32[]{:S(2)}) collective-permute-start(bf16[4,128,128]{2,1,0:T(8,128)(2,1)S(1)} %get-tuple-element.45), channel_id=1, source_target_pairs={{0,1},{1,0},{2,3},{3,2},{4,5},{5,4},{6,7},{7,6},{8,9},{9,8},{10,11... | collective-permute-start | bytes 393224 | tf_op jit(solution)/shard_map/ppermute | solution.py:546
  47.3 5.7 %attend.2 = (bf16[2,1024,256]{2,1,0:T(8,128)(2,1)S(1)}, bf16[2,1024,256]{2,1,0:T(8,128)(2,1)S(1)}) custom-call(s32[1]{0:T(128)} %bitcast.refs_0_, s32[1,128]{1,0:T(1,128)S(1)} %bitcast.10, bf16[1024,1024]{1,0:T(8,128)(2,1)} %refs_2_.5, bf16[1024,1024]{1,0:T(8,128)(2,1)} %refs_3_.5, bf16[1024,1024]{1,0:T(8,128)(2,1)} %refs_4_.5, ...), custom_call_target="tpu_custom_call" | custom-call | tf_op jit(solution)/shard_map/attend/pallas_call | solution.py:516
  53.0 0.0 copy-start.1
  53.0 5.0 %attend.3 = (bf16[2,1024,256]{2,1,0:T(8,128)(2,1)}, bf16[2,1024,256]{2,1,0:T(8,128)(2,1)}) custom-call(s32[1]{0:T(128)} %bitcast.refs_0_, s32[1,128]{1,0:T(1,128)S(1)} %bitcast.11, bf16[1024,1024]{1,0:T(8,128)(2,1)} %refs_2_.5, bf16[1024,1024]{1,0:T(8,128)(2,1)} %refs_3_.5, bf16[1024,1024]{1,0:T(8,128)(2,1)} %refs_4_.5, ...), custom_call_target="tpu_custom_call" | custom-call | tf_op jit(solution)/shard_map/attend/pallas_call | solution.py:516
  58.0 0.0 copy-done.1
  58.0 1.9 %finish.2 = (bf16[1024,1024]{1,0:T(8,128)(2,1)}, bf16[2,1024,256]{2,1,0:T(8,128)(2,1)S(1)}, bf16[2,1024,256]{2,1,0:T(8,128)(2,1)S(1)}) custom-call(s32[1]{0:T(128)} %bitcast.refs_0_, f32[48,128]{1,0:T(8,128)S(1)} %get-tuple-element.26.refs_1_.r_0_.gate_ref, bf16[2,1024,256]{2,1,0:T(8,128)(2,1)S(1)} %get-tuple-element.27.refs_2_, ...), custom_call_target="tpu_custom_call" | custom-call | tf_op jit(solution)/shard_map/finish/pallas_call | solution.py:552
  59.9 0.0 collective-permute-done.2.refs_5_
  59.9 1.9 %finish.3 = bf16[1024,1024]{1,0:T(8,128)(2,1)} custom-call(s32[1]{0:T(128)} %bitcast.refs_0_, f32[48,128]{1,0:T(8,128)S(1)} %get-tuple-element.26.refs_1_.r_0_.gate_ref, bf16[2,1024,256]{2,1,0:T(8,128)(2,1)S(1)} %get-tuple-element.42.refs_2_, bf16[2,1024,256]{2,1,0:T(8,128)(2,1)S(1)} %get-tuple-element.43.refs_3_, ...), custom_call_target="tpu_custom_call", output_to_operand_aliasing={{}: (7, {})} | custom-call | tf_op jit(solution)/shard_map/finish/pallas_call | solution.py:552
Async XLA Ops:
  0.0 3.8 %copy-start = (f32[3,4,1024]{2,1,0:T(4,128)S(1)}, f32[3,4,1024]{2,1,0:T(4,128)}, u32[]{:S(2)}) copy-start(f32[3,4,1024]{2,1,0:T(4,128)} %refs_6_.3) | copy-start | bytes 147460
  0.0 3.8 %copy-start.2 = (s32[128]{0:T(128)S(1)}, s32[128]{0:T(128)}, u32[]{:S(2)}) copy-start(s32[128]{0:T(128)} %param.9) | copy-start | bytes 1540
  0.8 8.7 %collective-permute-start = (bf16[3,8,1024]{2,1,0:T(8,128)(2,1)S(1)}, bf16[3,8,1024]{2,1,0:T(8,128)(2,1)S(1)}, u32[]{:S(2)}, u32[]{:S(2)}) collective-permute-start(bf16[3,8,1024]{2,1,0:T(8,128)(2,1)S(1)} %rim.1), channel_id=1, source_target_pairs={{0,1},{1,2},{2,3},{3,4},{4,5},{5,6},{6,7},{7,8},{8,9},{9,10},{10,1... | collective-permute-start | bytes 147464 | tf_op jit(solution)/shard_map/ppermute | solution.py:449
  10.4 3.1 %collective-permute-start.1 = (bf16[4,128,128]{2,1,0:T(8,128)(2,1)S(1)}, bf16[4,128,128]{2,1,0:T(8,128)(2,1)S(1)}, u32[]{:S(2)}, u32[]{:S(2)}) collective-permute-start(bf16[4,128,128]{2,1,0:T(8,128)(2,1)S(1)} %get-tuple-element.36), channel_id=1, source_target_pairs={{0,1},{1,0},{2,3},{3,2},{4,5},{5,4},{6,7},{7,6},{8,9},{9,8},{10,11... | collective-permute-start | bytes 393224 | tf_op jit(solution)/shard_map/ppermute | solution.py:506
  44.5 15.4 %collective-permute-start.2 = (bf16[4,128,128]{2,1,0:T(8,128)(2,1)S(1)}, bf16[4,128,128]{2,1,0:T(8,128)(2,1)S(1)}, u32[]{:S(2)}, u32[]{:S(2)}) collective-permute-start(bf16[4,128,128]{2,1,0:T(8,128)(2,1)S(1)} %get-tuple-element.45), channel_id=1, source_target_pairs={{0,1},{1,0},{2,3},{3,2},{4,5},{5,4},{6,7},{7,6},{8,9},{9,8},{10,11... | collective-permute-start | bytes 393224 | tf_op jit(solution)/shard_map/ppermute | solution.py:546
  53.0 5.0 %copy-start.1 = (f32[1024]{0:T(1024)S(1)}, f32[1024]{0:T(1024)}, u32[]{:S(2)}) copy-start(f32[1024]{0:T(1024)} %param.11) | copy-start | bytes 12292

commit v5 on v4

--- a/solution.py
+++ b/solution.py
@@ -3,15 +3,17 @@
 from jax import lax
 from jax.experimental import pallas as pl
 from jax.experimental.pallas import tpu as pltpu
-from jax.sharding import Mesh
 from jax.sharding import PartitionSpec as P
 
 HEAD = 128
 CHUNK = 256
 GROUP = 16
 BLOCK = 256
-CTX = ("x", "z", "c")
-DP_CTX = ("dp", "x", "z", "c")
+CTX = "ctx"
+DP_CTX = ("dp", "ctx")
+X_CHIPS = 4
+FIRST_X = 3
+FIRST_Z = 5
 F32 = jnp.float32
 BF16 = jnp.bfloat16
 
@@ -392,11 +394,12 @@
     out_ref[...] = (own_ref[...].astype(F32) * own + got_ref[...].astype(F32) * got).astype(BF16)
 
 
-def enter_kernel(gate_ref, spread_ref, out_ref):
+def enter_kernel(gate_ref, spread_ref, out_ref, *, counted):
     running = jnp.zeros(spread_ref.shape[1:], F32)
-    for n in range(spread_ref.shape[0]):
+    for chip in range(spread_ref.shape[0]):
+        n = counted.index(chip)
         out_ref[n] = running.astype(BF16)
-        running = running * gate_ref[n : n + 1] + spread_ref[n].astype(F32)
+        running = running * gate_ref[chip : chip + 1] + spread_ref[n].astype(F32)
 
 
 def carry_kernel(gate_ref, entered_ref, own_ref, got_ref, mine_ref, other_ref, *, chips):
@@ -430,10 +433,15 @@
     heads = channels // HEAD
     half = heads // 2
     chunks = rows // CHUNK
-    chips = lax.axis_size("x") * lax.axis_size("z")
-    ctx_count = 2 * chips
+    ctx_count = lax.axis_size(CTX)
+    chips = ctx_count // 2
+    z_chips = chips // X_CHIPS
+    counted = [
+        (FIRST_X + x) % X_CHIPS * z_chips + (FIRST_Z + z) % z_chips for x in range(X_CHIPS) for z in range(z_chips)
+    ]
+    groups = [[2 * chip + core for chip in counted] for core in (0, 1)]
     here = lax.axis_index(CTX).astype(jnp.int32).reshape(1)
-    swap = [(0, 1), (1, 0)]
+    swap = [(i, i ^ 1) for i in range(ctx_count)]
 
     smem = pl.BlockSpec(memory_space=pltpu.SMEM)
     last_rows = pl.BlockSpec((8, channels), lambda i: (rows // 8 - 1, 0))
@@ -503,12 +511,12 @@
         )(here, gates, key_head, value_head, inside, live, rims, conv_weight, st_late)
 
     inner_other, other = first(False)
-    got = lax.ppermute(other, "c", swap)
+    got = lax.ppermute(other, CTX, swap)
     inner_own, own = first(True)
 
     state = (half, HEAD, HEAD)
     chip_tail = small(lambda *r: join_kernel(*r, chips=chips), shaped(*state), gates, own, got)
-    spread = lax.all_to_all(chip_tail.reshape(chips, -1, HEAD), ("x", "z"), 0, 0, tiled=True)
+    spread = lax.all_to_all(chip_tail.reshape(chips, -1, HEAD), CTX, 0, 0, axis_index_groups=groups, tiled=True)
 
     def attend(mine, *ready):
         shape = (half_pairs, rows, 2 * HEAD)
@@ -538,12 +546,12 @@
     phi_other, mix_other = (in_hbm(x) for x in attend(False, pk_late, val_late))
     phi_own, mix_own = attend(True)
 
-    entering = small(enter_kernel, shaped(*spread.shape), gates, spread)
-    entered = lax.all_to_all(entering, ("x", "z"), 0, 0, tiled=True).reshape(state)
+    entering = small(lambda *r: enter_kernel(*r, counted=counted), shaped(*spread.shape), gates, spread)
+    entered = lax.all_to_all(entering, CTX, 0, 0, axis_index_groups=groups, tiled=True).reshape(state)
     carried_own, carried_other = small(
         lambda *r: carry_kernel(*r, chips=chips), [shaped(*state)] * 2, gates, entered, own, got
     )
-    carried_far = lax.ppermute(carried_other, "c", swap)
+    carried_far = lax.ppermute(carried_other, CTX, swap)
 
     def finish(mine, phi, mix, inner, carried, *others):
         shape = (half_pairs, rows, 2 * HEAD)
@@ -568,11 +576,9 @@
 
 
 def solution(mesh):
-    finer = Mesh(mesh.devices.reshape(mesh.shape["dp"], 4, 8, 2), DP_CTX)
-
     return jax.shard_map(
         per_device,
-        mesh=finer,
+        mesh=mesh,
         in_specs=(P(DP_CTX, None), P(DP_CTX, None), P(DP_CTX, None), P("dp"), P(), P()),
         out_specs=P(DP_CTX, None),
         check_vma=False,

time: 62 us -> 59.5 us (0.960)
  blocking collectives: 30.8 us -> 28.7 us
    all_to_all x2, blocking collectives: 30.8 us -> 28.7 us  [the longest x1 16 us: per_device(): lax.all_to_all(chip_tail.reshape(chips, -1, HEAD), CTX, 0, 0, axis_index_...]
  transfers between devices with their start and end apart: 3 -> 3, of which waited for: 1 -> 1; matrix products, arithmetic and copies ran while one was open for 0% -> 0% of each run, Pallas kernels for 31% -> 32%
where the time goes in v5:
time: 59.5 us; the launch traced here: 59.2 us
  blocking collectives  28.7 us (48%)
  Pallas kernels  22.9 us (38%)
  starting transfers between devices  7.5 us (13%)
    all_to_all x1, blocking collectives, per_device(): lax.all_to_all(chip_tail.reshape(chips, -1, HEAD), CTX, 0, 0, axis_index_...  16 us
    all_to_all x1, blocking collectives, per_device(): lax.all_to_all(entering, CTX, 0, 0, axis_index_groups=groups, tiled=True)  12.7 us
    pallas_call x2, Pallas kernels, attend(): pl.pallas_call(lambda *refs: attend_kernel(*refs, mine=mine), in_specs=[s...  10.7 us
    pallas_call x1, Pallas kernels, per_device(): pl.pallas_call(lambda *refs: late_kernel(*refs, chips=chips), in_specs=[s...  5.66 us
    pallas_call x2, Pallas kernels, finish(): pl.pallas_call(lambda *refs: finish_kernel(*refs, mine=mine, chips=chips)...  3.73 us
    ppermute x1, starting transfers between devices, per_device(): lax.ppermute(rims, CTX, [(i, (i + 1) % ctx_count) for i in range(ctx_coun...  3.02 us
    ppermute x1, starting transfers between devices, per_device(): carried_far = lax.ppermute(carried_other, CTX, swap)  2.34 us
    ppermute x1, starting transfers between devices, per_device(): got = lax.ppermute(other, CTX, swap)  2.14 us
  transfers between devices with their start and end apart: 3, of which 1 were waited for; matrix products, arithmetic and copies ran while one was open for 0% of the time, Pallas kernels for 32%

profile of v5, /device:TPU:1, one launch (start us, length us, event | category | flops | bytes accessed | tf_op | source)
XLA Modules:
  0.0 59.2 jit_solution(13327790727366240972)
XLA Ops:
  0.0 0.0 copy-start
  0.0 0.0 copy-start.2
  0.0 0.8 %rim.1 = bf16[3,8,1024]{2,1,0:T(8,128)(2,1)S(1)} custom-call(bf16[1024,1024]{1,0:T(8,128)(2,1)} %refs_2_.5, bf16[1024,1024]{1,0:T(8,128)(2,1)} %refs_3_.5, bf16[1024,1024]{1,0:T(8,128)(2,1)} %refs_4_.5), custom_call_target="tpu_custom_call" | custom-call | tf_op jit(solution)/shard_map/rim/pallas_call | solution.py:448
  0.8 3.0 %collective-permute-start = (bf16[3,8,1024]{2,1,0:T(8,128)(2,1)S(1)}, bf16[3,8,1024]{2,1,0:T(8,128)(2,1)S(1)}, u32[]{:S(2)}, u32[]{:S(2)}) collective-permute-start(bf16[3,8,1024]{2,1,0:T(8,128)(2,1)S(1)} %rim.1), channel_id=1, source_target_pairs={{0,1},{1,2},{2,3},{3,4},{4,5},{5,6},{6,7},{7,8},{8,9},{9,10},{10,1... | collective-permute-start | bytes 147464 | tf_op jit(solution)/shard_map/ppermute | solution.py:457
  3.8 0.0 copy-done
  3.8 0.0 copy-done.2
  3.8 5.7 %late.1 = (bf16[4,768,128]{2,1,0:T(8,128)(2,1)}, bf16[4,768,128]{2,1,0:T(8,128)(2,1)}, f32[8,3,128,128]{3,2,1,0:T(8,128)S(1)}, f32[48,128]{1,0:T(8,128)S(1)}, bf...) custom-call(s32[1]{0:T(128)} %bitcast.refs_0_, ...), custom_call_target="tpu_custom_call" | custom-call | tf_op jit(solution)/shard_map/late/pallas_call | solution.py:475
  9.5 0.0 collective-permute-done.refs_5_.refs_6_
  9.5 0.9 %first.3 = (bf16[4,3,128,128]{3,2,1,0:T(8,128)(2,1)S(1)}, bf16[4,128,128]{2,1,0:T(8,128)(2,1)S(1)}) custom-call(s32[1]{0:T(128)} %bitcast.refs_0_, f32[48,128]{1,0:T(8,128)S(1)} %get-tuple-element.26.refs_1_.r_0_, bf16[256,1024]{1,0:T(8,128)(2,1)S(1)} %get-tuple-element.29.refs_2_, bf16[256,1024]{1,0:T(8,128)(2,1)S(1)} %get-tuple-element.30.refs_3_, ...), custom_call_target="tpu_custom_call" | custom-call | tf_op jit(solution)/shard_map/first/pallas_call | solution.py:500
  10.4 2.1 %collective-permute-start.1 = (bf16[4,128,128]{2,1,0:T(8,128)(2,1)S(1)}, bf16[4,128,128]{2,1,0:T(8,128)(2,1)S(1)}, u32[]{:S(2)}, u32[]{:S(2)}) collective-permute-start(bf16[4,128,128]{2,1,0:T(8,128)(2,1)S(1)} %get-tuple-element.36), channel_id=1, source_target_pairs={{0,1},{1,0},{2,3},{3,2},{4,5},{5,4},{6,7},{7,6},{8,9},{9,8},{10,11... | collective-permute-start | bytes 393224 | tf_op jit(solution)/shard_map/ppermute | solution.py:514
  12.5 0.9 %first.2 = (bf16[4,3,128,128]{3,2,1,0:T(8,128)(2,1)S(1)}, bf16[4,128,128]{2,1,0:T(8,128)(2,1)S(1)}) custom-call(s32[1]{0:T(128)} %bitcast.refs_0_, f32[48,128]{1,0:T(8,128)S(1)} %get-tuple-element.26.refs_1_.r_0_, bf16[256,1024]{1,0:T(8,128)(2,1)S(1)} %get-tuple-element.29.refs_2_, bf16[256,1024]{1,0:T(8,128)(2,1)S(1)} %get-tuple-element.30.refs_3_, ...), custom_call_target="tpu_custom_call" | custom-call | tf_op jit(solution)/shard_map/first/pallas_call | solution.py:500
  13.4 0.1 collective-permute-done.1.r_2_.r_3_
  13.5 0.1 shard_map.64
  13.6 16.0 %all_to_all.10.r_1_ = bf16[32,16,128]{2,1,0:T(8,128)(2,1)S(1)} all-to-all(bf16[32,16,128]{2,1,0:T(8,128)(2,1)S(1)} %bitcast.6), channel_id=1, replica_groups={{58,60,62,48,50,52,54,56,10,12,14,0,2,4,6,8,26,28,30,16,18,20,22,24,42,..., dimensions={0} | all-to-all | bytes 262144 | tf_op jit(solution)/shard_map/all_to_all | solution.py:519
  29.5 0.1 shard_map.65
  29.6 12.7 %all_to_all.11 = bf16[32,16,128]{2,1,0:T(8,128)(2,1)S(1)} all-to-all(bf16[32,16,128]{2,1,0:T(8,128)(2,1)S(1)} %shard_map.65), channel_id=1, replica_groups={{58,60,62,48,50,52,54,56,10,12,14,0,2,4,6,8,26,28,30,16,18,20,22,24,42,..., dimensions={0} | all-to-all | bytes 262144 | tf_op jit(solution)/shard_map/all_to_all | solution.py:550
  42.3 0.1 shard_map.66
  42.4 2.3 %collective-permute-start.2 = (bf16[4,128,128]{2,1,0:T(8,128)(2,1)S(1)}, bf16[4,128,128]{2,1,0:T(8,128)(2,1)S(1)}, u32[]{:S(2)}, u32[]{:S(2)}) collective-permute-start(bf16[4,128,128]{2,1,0:T(8,128)(2,1)S(1)} %get-tuple-element.45), channel_id=1, source_target_pairs={{0,1},{1,0},{2,3},{3,2},{4,5},{5,4},{6,7},{7,6},{8,9},{9,8},{10,11... | collective-permute-start | bytes 393224 | tf_op jit(solution)/shard_map/ppermute | solution.py:554
  44.7 5.7 %attend.2 = (bf16[2,1024,256]{2,1,0:T(8,128)(2,1)S(1)}, bf16[2,1024,256]{2,1,0:T(8,128)(2,1)S(1)}) custom-call(s32[1]{0:T(128)} %bitcast.refs_0_, s32[1,128]{1,0:T(1,128)S(1)} %bitcast.10, bf16[1024,1024]{1,0:T(8,128)(2,1)} %refs_2_.5, bf16[1024,1024]{1,0:T(8,128)(2,1)} %refs_3_.5, bf16[1024,1024]{1,0:T(8,128)(2,1)} %refs_4_.5, ...), custom_call_target="tpu_custom_call" | custom-call | tf_op jit(solution)/shard_map/attend/pallas_call | solution.py:524
  50.5 0.0 copy-start.1
  50.5 5.0 %attend.3 = (bf16[2,1024,256]{2,1,0:T(8,128)(2,1)}, bf16[2,1024,256]{2,1,0:T(8,128)(2,1)}) custom-call(s32[1]{0:T(128)} %bitcast.refs_0_, s32[1,128]{1,0:T(1,128)S(1)} %bitcast.11, bf16[1024,1024]{1,0:T(8,128)(2,1)} %refs_2_.5, bf16[1024,1024]{1,0:T(8,128)(2,1)} %refs_3_.5, bf16[1024,1024]{1,0:T(8,128)(2,1)} %refs_4_.5, ...), custom_call_target="tpu_custom_call" | custom-call | tf_op jit(solution)/shard_map/attend/pallas_call | solution.py:524
  55.5 0.0 copy-done.1
  55.5 1.9 %finish.2 = (bf16[1024,1024]{1,0:T(8,128)(2,1)}, bf16[2,1024,256]{2,1,0:T(8,128)(2,1)S(1)}, bf16[2,1024,256]{2,1,0:T(8,128)(2,1)S(1)}) custom-call(s32[1]{0:T(128)} %bitcast.refs_0_, f32[48,128]{1,0:T(8,128)S(1)} %get-tuple-element.26.refs_1_.r_0_, bf16[2,1024,256]{2,1,0:T(8,128)(2,1)S(1)} %get-tuple-element.27.refs_2_, ...), custom_call_target="tpu_custom_call" | custom-call | tf_op jit(solution)/shard_map/finish/pallas_call | solution.py:560
  57.4 0.0 collective-permute-done.2.refs_5_
  57.4 1.9 %finish.3 = bf16[1024,1024]{1,0:T(8,128)(2,1)} custom-call(s32[1]{0:T(128)} %bitcast.refs_0_, f32[48,128]{1,0:T(8,128)S(1)} %get-tuple-element.26.refs_1_.r_0_, bf16[2,1024,256]{2,1,0:T(8,128)(2,1)S(1)} %get-tuple-element.42.refs_2_, bf16[2,1024,256]{2,1,0:T(8,128)(2,1)S(1)} %get-tuple-element.43.refs_3_, ...), custom_call_target="tpu_custom_call", output_to_operand_aliasing={{}: (7, {})} | custom-call | tf_op jit(solution)/shard_map/finish/pallas_call | solution.py:560
Async XLA Ops:
  0.0 3.8 %copy-start = (f32[3,4,1024]{2,1,0:T(4,128)S(1)}, f32[3,4,1024]{2,1,0:T(4,128)}, u32[]{:S(2)}) copy-start(f32[3,4,1024]{2,1,0:T(4,128)} %refs_6_.3) | copy-start | bytes 147460
  0.0 3.8 %copy-start.2 = (s32[128]{0:T(128)S(1)}, s32[128]{0:T(128)}, u32[]{:S(2)}) copy-start(s32[128]{0:T(128)} %param.9) | copy-start | bytes 1540
  0.8 8.7 %collective-permute-start = (bf16[3,8,1024]{2,1,0:T(8,128)(2,1)S(1)}, bf16[3,8,1024]{2,1,0:T(8,128)(2,1)S(1)}, u32[]{:S(2)}, u32[]{:S(2)}) collective-permute-start(bf16[3,8,1024]{2,1,0:T(8,128)(2,1)S(1)} %rim.1), channel_id=1, source_target_pairs={{0,1},{1,2},{2,3},{3,4},{4,5},{5,6},{6,7},{7,8},{8,9},{9,10},{10,1... | collective-permute-start | bytes 147464 | tf_op jit(solution)/shard_map/ppermute | solution.py:457
  10.4 3.1 %collective-permute-start.1 = (bf16[4,128,128]{2,1,0:T(8,128)(2,1)S(1)}, bf16[4,128,128]{2,1,0:T(8,128)(2,1)S(1)}, u32[]{:S(2)}, u32[]{:S(2)}) collective-permute-start(bf16[4,128,128]{2,1,0:T(8,128)(2,1)S(1)} %get-tuple-element.36), channel_id=1, source_target_pairs={{0,1},{1,0},{2,3},{3,2},{4,5},{5,4},{6,7},{7,6},{8,9},{9,8},{10,11... | collective-permute-start | bytes 393224 | tf_op jit(solution)/shard_map/ppermute | solution.py:514
  42.4 15.0 %collective-permute-start.2 = (bf16[4,128,128]{2,1,0:T(8,128)(2,1)S(1)}, bf16[4,128,128]{2,1,0:T(8,128)(2,1)S(1)}, u32[]{:S(2)}, u32[]{:S(2)}) collective-permute-start(bf16[4,128,128]{2,1,0:T(8,128)(2,1)S(1)} %get-tuple-element.45), channel_id=1, source_target_pairs={{0,1},{1,0},{2,3},{3,2},{4,5},{5,4},{6,7},{7,6},{8,9},{9,8},{10,11... | collective-permute-start | bytes 393224 | tf_op jit(solution)/shard_map/ppermute | solution.py:554
  50.5 5.0 %copy-start.1 = (f32[1024]{0:T(1024)S(1)}, f32[1024]{0:T(1024)}, u32[]{:S(2)}) copy-start(f32[1024]{0:T(1024)} %param.11) | copy-start | bytes 12292
